TPU v7x, 32 devices: a whole 2x2x4 slice. The times are simulated.
32 devices in a mesh: dp: 8 (over z, x), tensor: 4 (over y, core).
Axes of the slice: x: 2, y: 2, z: 4, core: 2. Of those that a mesh axis runs over, the one named last changes fastest.
Arguments:
- images_in: bfloat16 [32, 544, 768], P(('dp', 'tensor')), may hold values from -6 to 6
- crop_lengths: int32 [32, 6], P('dp'), may hold values from 1 to 197, 544 in all within a row
- route_index: int32 [32, 272], P('dp'), may hold values from 0 to 543, as said below
- router_weight: bfloat16 [768], replicated, may hold values from -0.21875 to 0.21875
- norm_gain: bfloat16 [2, 2, 768], replicated, may hold values from 0.5 to 1.5
- norm_shift: bfloat16 [2, 2, 768], replicated, may hold values from -1.75 to 1.75
- qkv_weight: bfloat16 [2, 3, 768, 768], P(None, None, None, 'tensor'), may hold values from -0.21875 to 0.21875
- qv_bias: bfloat16 [2, 2, 768], P(None, None, 'tensor'), may hold values from -3 to 3
- out_weight: bfloat16 [2, 768, 768], P(None, 'tensor'), may hold values from -0.75 to 0.75
- out_bias: bfloat16 [2, 768], replicated, may hold values from -1.75 to 1.75
- fc1_weight: bfloat16 [2, 768, 3072], P(None, None, 'tensor'), may hold values from -0.21875 to 0.21875
- fc1_bias: bfloat16 [2, 3072], P(None, 'tensor'), may hold values from -3 to 3
- fc2_weight: bfloat16 [2, 3072, 768], P(None, 'tensor'), may hold values from -0.109375 to 0.109375
- fc2_bias: bfloat16 [2, 768], replicated, may hold values from -1.75 to 1.75
- out_cotangent: bfloat16 [32, 544, 768], P(('dp', 'tensor')), may hold values from -6 to 6
Outputs:
- images_out: bfloat16 [32, 544, 768], P(('dp', 'tensor'))
- input_grad: float32 [32, 544, 768], P(('dp', 'tensor'))
- router_grad: float32 [768], replicated
- gain_grad: float32 [2, 2, 768], replicated
- shift_grad: float32 [2, 2, 768], replicated
- qkv_grad: float32 [2, 3, 768, 768], P(None, None, None, 'tensor')
- qv_bias_grad: float32 [2, 2, 768], P(None, None, 'tensor')
- out_weight_grad: float32 [2, 768, 768], P(None, 'tensor')
- out_bias_grad: float32 [2, 768], replicated
- fc1_grad: float32 [2, 768, 3072], P(None, None, 'tensor')
- fc1_bias_grad: float32 [2, 3072], P(None, 'tensor')
- fc2_grad: float32 [2, 3072, 768], P(None, 'tensor')
- fc2_bias_grad: float32 [2, 768], replicated
Inputs may be any that keep to these rules, and one draw needn't show every extreme that they name: `route_index`: within each image the 272 positions are distinct and ascending.
All inputs are finite; a program needn't handle non-finite values.
Results may differ from a plain program's by a relative error of at most 0.02.
Values may be sent and summed in bfloat16 or wider, within the bound.
A program may use at most 256 MiB of HBM per device.

v0:
```python
import jax
import jax.numpy as jnp
from jax import lax
from jax.sharding import PartitionSpec as P

HEAD_DIM = 64


norm_eps = 1e-06
mask_fill = -1e30
half_root = 0.7071067811865476
inv_root_tau = 0.3989422804014327


def crop_index(lengths, positions):
    bounds = jnp.cumsum(lengths, axis=-1)
    above = positions[:, :, None] >= bounds[:, None, :]
    return jnp.sum(above.astype(jnp.int32), axis=-1)


def norm_rows(inputs, gain_row, shift_row):
    row_mean = jnp.mean(inputs, axis=-1, keepdims=True)
    centred = inputs - row_mean
    inv_std = lax.rsqrt(jnp.mean(centred * centred, axis=-1, keepdims=True) + norm_eps)
    normalised = centred * inv_std
    return (normalised, inv_std, (normalised * gain_row + shift_row).astype(jnp.bfloat16))


def norm_back(gradient, normalised, inv_std, gain_row):
    features = gradient.shape[-1]
    scaled = gradient * gain_row
    inner = jnp.mean(scaled, axis=-1, keepdims=True) + normalised * jnp.mean(
        scaled * normalised, axis=-1, keepdims=True
    )
    gain_part = jnp.sum((gradient * normalised).reshape(-1, features), axis=0)
    shift_part = jnp.sum(gradient.reshape(-1, features), axis=0)
    return (inv_std * (scaled - inner), gain_part, shift_part)


def gelu_value(preact):
    return 0.5 * preact * (1.0 + lax.erf(preact * half_root))


def gelu_slope(preact):
    return 0.5 * (1.0 + lax.erf(preact * half_root)) + preact * inv_root_tau * jnp.exp(
        -0.5 * preact * preact
    )


def block_images(images_all, length):
    per_block = 1
    while per_block * length < 512 and images_all % (2 * per_block) == 0:
        per_block = per_block * 2
    return per_block


def by_blocks(function, arrays, per_block):
    shaped = jax.tree.map(
        lambda item: item.reshape((item.shape[0] // per_block, per_block) + item.shape[1:]), arrays
    )
    result = lax.map(function, shaped)
    return jax.tree.map(
        lambda item: item.reshape((item.shape[0] * item.shape[1],) + item.shape[2:]), result
    )


def masked_scores(queries, key_rows, crops):
    scale = queries.shape[-1] ** (-0.5)
    raw_scores = (
        jnp.einsum("gqhe,gkhe->ghqk", queries, key_rows, preferred_element_type=jnp.float32) * scale
    )
    same_crop = (crops[:, :, None] == crops[:, None, :])[:, None]
    return jnp.where(same_crop, raw_scores, mask_fill)


def attend_block(block_parts):
    queries, key_rows, values, crops = block_parts
    scores = masked_scores(queries, key_rows, crops)
    row_max = jnp.max(scores, axis=-1, keepdims=True)
    exponent = jnp.exp(scores - row_max)
    row_total = jnp.sum(exponent, axis=-1, keepdims=True)
    attn_probs = (exponent / row_total).astype(jnp.bfloat16)
    head_out = jnp.einsum("ghqk,gkhe->gqhe", attn_probs, values, preferred_element_type=jnp.float32)
    return (head_out.astype(jnp.bfloat16), (row_max + jnp.log(row_total))[..., 0])


def attend_back(block_parts):
    queries, key_rows, values, head_grads, log_total, crops = block_parts
    scale = queries.shape[-1] ** (-0.5)
    scores = masked_scores(queries, key_rows, crops)
    attn_probs = jnp.exp(scores - log_total[..., None])
    low_probs = attn_probs.astype(jnp.bfloat16)
    value_grad = jnp.einsum(
        "ghqk,gqhe->gkhe", low_probs, head_grads, preferred_element_type=jnp.float32
    )
    prob_grad = jnp.einsum(
        "gqhe,gkhe->ghqk", head_grads, values, preferred_element_type=jnp.float32
    )
    score_grad = (
        attn_probs * (prob_grad - jnp.sum(attn_probs * prob_grad, axis=-1, keepdims=True))
    ).astype(jnp.bfloat16)
    query_grad = (
        jnp.einsum("ghqk,gkhe->gqhe", score_grad, key_rows, preferred_element_type=jnp.float32)
        * scale
    )
    key_grad = (
        jnp.einsum("ghqk,gqhe->gkhe", score_grad, queries, preferred_element_type=jnp.float32)
        * scale
    )
    return (
        query_grad.astype(jnp.bfloat16),
        key_grad.astype(jnp.bfloat16),
        value_grad.astype(jnp.bfloat16),
    )


def attention_forward(
    inputs, crops_all, gain_row, shift_row, qkv_weights, qv_biases, out_weights, out_biases
):
    normalised, inv_std, normed = norm_rows(inputs, gain_row, shift_row)
    gathered = lax.all_gather(normed, "tensor", axis=0, tiled=True)
    images_all, length, features = gathered.shape
    local_width = qkv_weights.shape[-1]
    head_shape = (images_all, length, local_width // HEAD_DIM, HEAD_DIM)
    projected = jnp.einsum(
        "gld,cde->glce", gathered, qkv_weights, preferred_element_type=jnp.float32
    )
    queries = (projected[:, :, 0] + qv_biases[0]).astype(jnp.bfloat16).reshape(head_shape)
    key_rows = projected[:, :, 1].astype(jnp.bfloat16).reshape(head_shape)
    values = (projected[:, :, 2] + qv_biases[1]).astype(jnp.bfloat16).reshape(head_shape)
    per_block = block_images(images_all, length)
    head_out, log_total = by_blocks(attend_block, (queries, key_rows, values, crops_all), per_block)
    head_out = head_out.reshape(images_all, length, local_width)
    branch = (
        lax.psum_scatter(
            jnp.einsum("gle,ed->gld", head_out, out_weights, preferred_element_type=jnp.float32),
            "tensor",
            scatter_dimension=0,
            tiled=True,
        )
        + out_biases
    )
    out_keep = (head_out, out_weights)
    kept = (normalised, inv_std, gathered, queries, key_rows, values, log_total, out_keep)
    return (branch, kept)


def attention_back(gradient, kept, crops_all, gain_row, qkv_weights):
    normalised, inv_std, gathered, queries, key_rows, values, log_total, out_keep = kept
    own_count, length, features = gradient.shape
    grad_low = gradient.astype(jnp.bfloat16)
    out_bias_part = jnp.sum(grad_low.reshape(-1, features), axis=0, dtype=jnp.float32)
    images_all = queries.shape[0]
    local_width = queries.shape[2] * queries.shape[3]
    head_out, out_weights = out_keep
    grad_all = lax.all_gather(grad_low, "tensor", axis=0, tiled=True)
    out_part = jnp.einsum("gle,gld->ed", head_out, grad_all, preferred_element_type=jnp.float32)
    head_grads = jnp.einsum(
        "gld,ed->gle", grad_all, out_weights, preferred_element_type=jnp.float32
    )
    head_grads = head_grads.astype(jnp.bfloat16).reshape(queries.shape)
    per_block = block_images(images_all, length)
    query_grad, key_grad, value_grad = by_blocks(
        attend_back, (queries, key_rows, values, head_grads, log_total, crops_all), per_block
    )
    qv_part = jnp.stack(
        [
            jnp.sum(query_grad.reshape(-1, local_width), axis=0, dtype=jnp.float32),
            jnp.sum(value_grad.reshape(-1, local_width), axis=0, dtype=jnp.float32),
        ]
    )
    proj_grad = jnp.stack([query_grad, key_grad, value_grad], axis=2).reshape(
        images_all, length, 3, local_width
    )
    qkv_part = jnp.einsum("gld,glce->cde", gathered, proj_grad, preferred_element_type=jnp.float32)
    normed_grad = lax.psum_scatter(
        jnp.einsum(
            "glce,cde->gld", proj_grad, qkv_weights, preferred_element_type=jnp.float32
        ).astype(jnp.bfloat16),
        "tensor",
        scatter_dimension=0,
        tiled=True,
    ).astype(jnp.float32)
    input_part, gain_part, shift_part = norm_back(normed_grad, normalised, inv_std, gain_row)
    return (input_part, (gain_part, shift_part, qkv_part, qv_part, out_part, out_bias_part))


def dense_forward(
    inputs, gain_row, shift_row, first_weights, first_biases, second_weights, second_biases
):
    normalised, inv_std, normed = norm_rows(inputs, gain_row, shift_row)
    full_first, full_first_bias, full_second = (
        lax.all_gather(first_weights, "tensor", axis=1, tiled=True),
        lax.all_gather(first_biases, "tensor", axis=0, tiled=True),
        lax.all_gather(second_weights, "tensor", axis=0, tiled=True),
    )
    preact = (
        jnp.einsum("gld,df->glf", normed, full_first, preferred_element_type=jnp.float32)
        + full_first_bias
    )
    hidden = gelu_value(preact).astype(jnp.bfloat16)
    branch = (
        jnp.einsum("glf,fd->gld", hidden, full_second, preferred_element_type=jnp.float32)
        + second_biases
    )
    kept = (normalised, inv_std, normed, preact, hidden, full_first, full_second)
    return (branch, kept)


def dense_back(gradient, kept, gain_row):
    normalised, inv_std, normed, preact, hidden, first_weights, second_weights = kept
    own_count, length, features = gradient.shape
    grad_low = gradient.astype(jnp.bfloat16)
    second_bias_part = jnp.sum(grad_low.reshape(-1, features), axis=0, dtype=jnp.float32)
    second_part = jnp.einsum("glf,gld->fd", hidden, grad_low, preferred_element_type=jnp.float32)
    hidden_grad = jnp.einsum(
        "gld,fd->glf", grad_low, second_weights, preferred_element_type=jnp.float32
    )
    pre_grad = (hidden_grad * gelu_slope(preact)).astype(jnp.bfloat16)
    first_bias_part = jnp.sum(pre_grad.reshape(-1, pre_grad.shape[-1]), axis=0, dtype=jnp.float32)
    first_part = jnp.einsum("gld,glf->df", normed, pre_grad, preferred_element_type=jnp.float32)
    normed_grad = jnp.einsum(
        "glf,df->gld", pre_grad, first_weights, preferred_element_type=jnp.float32
    )
    first_part, first_bias_part, second_part = (
        lax.psum_scatter(
            first_part.astype(jnp.bfloat16), "tensor", scatter_dimension=1, tiled=True
        ).astype(jnp.float32),
        lax.psum_scatter(
            first_bias_part.astype(jnp.bfloat16), "tensor", scatter_dimension=0, tiled=True
        ).astype(jnp.float32),
        lax.psum_scatter(
            second_part.astype(jnp.bfloat16), "tensor", scatter_dimension=0, tiled=True
        ).astype(jnp.float32),
    )
    input_part, gain_part, shift_part = norm_back(normed_grad, normalised, inv_std, gain_row)
    return (
        input_part,
        (gain_part, shift_part, first_part, first_bias_part, second_part, second_bias_part),
    )


def body(
    images_in,
    crop_lengths,
    route_index,
    router_weight,
    norm_gain,
    norm_shift,
    qkv_weight,
    qv_bias,
    out_weight,
    out_bias,
    fc1_weight,
    fc1_bias,
    fc2_weight,
    fc2_bias,
    out_cotangent,
):
    own_count, length, features = images_in.shape
    images_all = crop_lengths.shape[0]
    offset = lax.axis_index("tensor") * own_count
    positions = jnp.broadcast_to(jnp.arange(length, dtype=jnp.int32), (images_all, length))
    crops_full = crop_index(crop_lengths, positions)
    crops_chosen = jnp.take_along_axis(crops_full, route_index, axis=1)
    own_index = lax.dynamic_slice_in_dim(route_index, offset, own_count, 0)
    row_index = jnp.arange(own_count, dtype=jnp.int32)[:, None]
    chosen = images_in[row_index, own_index]
    chosen_data = chosen.astype(jnp.float32)
    router_data = router_weight.astype(jnp.float32)
    router_logit = jnp.einsum(
        "nsd,d->ns", chosen, router_weight, preferred_element_type=jnp.float32
    )
    route_rate = 1.0 / (1.0 + jnp.exp(-router_logit))
    attn_one, kept_one = attention_forward(
        chosen_data,
        crops_chosen,
        norm_gain[0, 0],
        norm_shift[0, 0],
        qkv_weight[0],
        qv_bias[0],
        out_weight[0],
        out_bias[0],
    )
    middle = chosen_data + attn_one
    ffn_one, kept_two = dense_forward(
        middle,
        norm_gain[0, 1],
        norm_shift[0, 1],
        fc1_weight[0],
        fc1_bias[0],
        fc2_weight[0],
        fc2_bias[0],
    )
    branches = attn_one + ffn_one
    routed = (
        images_in.astype(jnp.float32)
        .at[row_index, own_index]
        .add(route_rate[:, :, None] * branches)
    )
    attn_two, kept_three = attention_forward(
        routed,
        crops_full,
        norm_gain[1, 0],
        norm_shift[1, 0],
        qkv_weight[1],
        qv_bias[1],
        out_weight[1],
        out_bias[1],
    )
    after_attn = routed + attn_two
    ffn_two, kept_four = dense_forward(
        after_attn,
        norm_gain[1, 1],
        norm_shift[1, 1],
        fc1_weight[1],
        fc1_bias[1],
        fc2_weight[1],
        fc2_bias[1],
    )
    images_out = (after_attn + ffn_two).astype(jnp.bfloat16)
    cotangent = out_cotangent.astype(jnp.float32)
    back_four, grads_four = dense_back(cotangent, kept_four, norm_gain[1, 1])
    grad_after = cotangent + back_four
    back_three, grads_three = attention_back(
        grad_after, kept_three, crops_full, norm_gain[1, 0], qkv_weight[1]
    )
    grad_routed = grad_after + back_three
    grad_chosen = grad_routed[row_index, own_index]
    logit_grad = jnp.sum(grad_chosen * branches, axis=-1) * route_rate * (1.0 - route_rate)
    router_part = jnp.einsum("nsd,ns->d", chosen_data, logit_grad, precision=lax.Precision.HIGHEST)
    branch_grad = route_rate[:, :, None] * grad_chosen
    back_two, grads_two = dense_back(branch_grad, kept_two, norm_gain[0, 1])
    back_one, grads_one = attention_back(
        branch_grad + back_two, kept_one, crops_chosen, norm_gain[0, 0], qkv_weight[0]
    )
    own_grad = logit_grad[:, :, None] * router_data + back_two + back_one
    input_grad = grad_routed.at[row_index, own_index].add(own_grad)
    gain_part = jnp.stack(
        [jnp.stack([grads_one[0], grads_two[0]]), jnp.stack([grads_three[0], grads_four[0]])]
    )
    shift_part = jnp.stack(
        [jnp.stack([grads_one[1], grads_two[1]]), jnp.stack([grads_three[1], grads_four[1]])]
    )
    out_bias_part = jnp.stack([grads_one[5], grads_three[5]])
    second_bias_part = jnp.stack([grads_two[5], grads_four[5]])
    shared = lax.psum(
        (router_part, gain_part, shift_part, out_bias_part, second_bias_part), ("dp", "tensor")
    )
    qkv_part = jnp.stack([grads_one[2], grads_three[2]])
    qv_part = jnp.stack([grads_one[3], grads_three[3]])
    out_part = jnp.stack([grads_one[4], grads_three[4]])
    first_part = jnp.stack([grads_two[2], grads_four[2]])
    first_bias_part = jnp.stack([grads_two[3], grads_four[3]])
    second_part = jnp.stack([grads_two[4], grads_four[4]])
    split = (
        lax.psum(qkv_part.astype(jnp.bfloat16), "dp").astype(jnp.float32),
        lax.psum(qv_part.astype(jnp.bfloat16), "dp").astype(jnp.float32),
        lax.psum(out_part.astype(jnp.bfloat16), "dp").astype(jnp.float32),
        lax.psum(first_part.astype(jnp.bfloat16), "dp").astype(jnp.float32),
        lax.psum(first_bias_part.astype(jnp.bfloat16), "dp").astype(jnp.float32),
        lax.psum(second_part.astype(jnp.bfloat16), "dp").astype(jnp.float32),
    )
    return (
        images_out,
        input_grad,
        shared[0],
        shared[1],
        shared[2],
        split[0],
        split[1],
        split[2],
        shared[3],
        split[3],
        split[4],
        split[5],
        shared[4],
    )


def solution(mesh):
    in_specs = (
        P(("dp", "tensor"), None, None),
        P("dp", None),
        P("dp", None),
        P(),
        P(),
        P(),
        P(None, None, None, "tensor"),
        P(None, None, "tensor"),
        P(None, "tensor", None),
        P(),
        P(None, None, "tensor"),
        P(None, "tensor"),
        P(None, "tensor", None),
        P(),
        P(("dp", "tensor"), None, None),
    )
    out_specs = (
        P(("dp", "tensor"), None, None),
        P(("dp", "tensor"), None, None),
        P(),
        P(),
        P(),
        P(None, None, None, "tensor"),
        P(None, None, "tensor"),
        P(None, "tensor", None),
        P(),
        P(None, None, "tensor"),
        P(None, "tensor"),
        P(None, "tensor", None),
        P(),
    )
    return jax.shard_map(body, mesh=mesh, in_specs=in_specs, out_specs=out_specs, check_vma=False)
```

profile of v0, /device:TPU:0, one launch (start us, length us, event | category | flops | bytes accessed | tf_op | source)
XLA Modules:
  0.0 1083.3 jit_solution(4589102543825514392)
XLA Ops:
  8.0 13.7 %gather_fusion = bf16[272,768]{1,0:T(8,128)(2,1)S(1)} fusion(bf16[1,544,768]{2,1,0:T(8,128)(2,1)} %param.23, s32[272]{0:T(512)S(1)} %get-tuple-element.320), kind=kCustom, calls=%fused_computation | custom fusion | bytes 837760 | tf_op jit(solution)/shard_map/gather | solution.py:268
  24.1 9.3 gather_fusion.2
  33.6 12.8 %all-gather.15.cloned.1.call-done = bf16[4,272,768]{2,1,0:T(8,128)(2,1)} async-done(((bf16[1,272,768]{2,1,0:T(8,128)(2,1)}), bf16[4,272,768]{2,1,0:T(8,128)(2,1)}) %all-gather.15.cloned.1.call-update) | async-done | bytes 1671184 | tf_op jit(solution)/shard_map/all_gather | solution.py:121
  55.6 5.0 while.52
  66.6 3.2 fusion.272
  69.9 5.4 all-gather.1
  76.4 26.0 %reduce-scatter.9.cloned.1.call-done = f32[1,272,768]{2,1,0:T(8,128)} async-done(((f32[4,272,768]{2,1,0:T(8,128)}), f32[1,272,768]{2,1,0:T(8,128)}) %reduce-scatter.9.cloned.1.call-update) | async-done | bytes 835600 | tf_op jit(solution)/shard_map/reduce_scatter | solution.py:135
  104.1 38.0 %all-gather.23.cloned.1.call-done = bf16[1,768,3072]{2,1,0:T(8,128)(2,1)} async-done(((bf16[1,768,768]{2,1,0:T(8,128)(2,1)}), bf16[1,768,3072]{2,1,0:T(8,128)(2,1)}) %all-gather.23.cloned.1.call-update) | async-done | bytes 4718608 | tf_op jit(solution)/shard_map/all_gather | solution.py:193
  142.2 6.1 multiply_convert_fusion.3
  148.3 33.4 %all-gather.25.cloned.1.call-done = bf16[1,3072,768]{2,1,0:T(8,128)(2,1)} async-done(((bf16[1,768,768]{2,1,0:T(8,128)(2,1)}), bf16[1,3072,768]{2,1,0:T(8,128)(2,1)}) %all-gather.25.cloned.1.call-update) | async-done | bytes 4718608 | tf_op jit(solution)/shard_map/all_gather | solution.py:195
  181.7 4.5 fusion.184
  191.6 29.3 %all-gather.17.cloned.1.call-done = bf16[4,544,768]{2,1,0:T(8,128)(2,1)} async-done(((bf16[1,544,768]{2,1,0:T(8,128)(2,1)}), bf16[4,544,768]{2,1,0:T(8,128)(2,1)}) %all-gather.17.cloned.1.call-update) | async-done | bytes 3342352 | tf_op jit(solution)/shard_map/all_gather | solution.py:121
  221.0 4.7 fusion.147
  229.4 25.0 %while.53 = (s32[]{:T(128)}, bf16[4,1,544,3,64]{2,4,3,1,0:T(8,128)(2,1)}, f32[4,1,3,544]{3,2,1,0:T(4,128)S(1)}, bf16[4,1,544,3,64]{2,4,3,1,0:T(8,128)(2,1)}, s32...) while((s32[]{:T(128)}, ...), condition=%wide.region_17.18_spmd, body=%wide.region_14.17_spmd.sunk | while | flops 238331296 | bytes 12944741 | solution.py:61
  254.4 5.1 fusion.243
  261.1 5.6 all-gather.4
  266.7 53.9 %reduce-scatter.11.cloned.1.call-done = f32[1,544,768]{2,1,0:T(8,128)} async-done(((f32[4,544,768]{2,1,0:T(8,128)}), f32[1,544,768]{2,1,0:T(8,128)}) %reduce-scatter.11.cloned.1.call-update) | async-done | bytes 1671184 | tf_op jit(solution)/shard_map/reduce_scatter | solution.py:135
  323.9 36.4 %all-gather.27.cloned.1.call-done = bf16[1,768,3072]{2,1,0:T(8,128)(2,1)} async-done(((bf16[1,768,768]{2,1,0:T(8,128)(2,1)}), bf16[1,768,3072]{2,1,0:T(8,128)(2,1)}) %all-gather.27.cloned.1.call-update) | async-done | bytes 4718608 | tf_op jit(solution)/shard_map/all_gather | solution.py:193
  360.3 8.7 multiply_convert_fusion.2
  368.9 31.0 %all-gather.29.cloned.1.call-done = bf16[1,3072,768]{2,1,0:T(8,128)(2,1)} async-done(((bf16[1,768,768]{2,1,0:T(8,128)(2,1)}), bf16[1,3072,768]{2,1,0:T(8,128)(2,1)}) %all-gather.29.cloned.1.call-update) | async-done | bytes 4718608 | tf_op jit(solution)/shard_map/all_gather | solution.py:195
  399.9 8.4 fusion.275
  408.3 3.6 fusion.160
  415.7 29.6 %all-gather.19.cloned.1.call-done = bf16[4,544,768]{2,1,0:T(8,128)(2,1)} async-done(((bf16[1,544,768]{2,1,0:T(8,128)(2,1)}), bf16[4,544,768]{2,1,0:T(8,128)(2,1)}) %all-gather.19.cloned.1.call-update) | async-done | bytes 3342352 | tf_op jit(solution)/shard_map/all_gather | solution.py:156
  445.3 4.1 convolution_convert_fusion.4
  452.7 45.8 %while.54 = (s32[]{:T(128)}, bf16[4,1,544,3,64]{2,4,3,1,0:T(8,128)(2,1)}, bf16[4,1,544,3,64]{2,4,3,1,0:T(8,128)(2,1)}, bf16[4,1,544,3,64]{2,4,3,1,0:T(8,128)(2,1...) while((s32[]{:T(128)}, ...), condition=%wide.region_25.26_spmd, body=%wide.region_23.25_spmd.sunk | while | flops 582330752 | bytes 35354008 | solution.py:61
  498.5 6.6 bitcast_convert_fusion
  505.5 39.1 %reduce-scatter.13.cloned.1.call-done = bf16[1,544,768]{2,1,0:T(8,128)(2,1)} async-done(((bf16[4,544,768]{2,1,0:T(8,128)(2,1)}), bf16[1,544,768]{2,1,0:T(8,128)(2,1)}) %reduce-scatter.13.cloned.1.call-update) | async-done | bytes 835600 | tf_op jit(solution)/shard_map/reduce_scatter | solution.py:176
  548.6 4.3 gather_fusion.1
  553.9 7.1 fusion.276
  561.0 5.2 fusion.216
  568.8 7.7 convolution_convert_fusion.3
  577.7 6.0 convolution_convert_fusion.1
  584.9 7.6 convolution_convert_fusion.2
  593.5 6.2 convolution_convert_fusion
  608.3 13.0 %while.55 = (s32[]{:T(128)}, bf16[2,2,272,3,64]{2,4,3,1,0:T(8,128)(2,1)}, bf16[2,2,272,3,64]{2,4,3,1,0:T(8,128)(2,1)}, bf16[2,2,272,3,64]{2,4,3,1,0:T(8,128)(2,1...) while((s32[]{:T(128)}, ...), condition=%wide.region_34.35_spmd, body=%wide.region_32.34_spmd.sunk | while | flops 288762272 | bytes 28893860 | solution.py:61
  625.3 4.1 bitcast_convert_fusion.1
  629.8 3.3 fusion.190
  641.2 50.0 %reduce-scatter.17.cloned.1.call-done = bf16[768,768]{1,0:T(8,128)(2,1)} async-done(((bf16[768,3072]{1,0:T(8,128)(2,1)}), bf16[768,768]{1,0:T(8,128)(2,1)}) %reduce-scatter.17.cloned.1.call-update) | async-done | bytes 1179664 | tf_op jit(solution)/shard_map/reduce_scatter | solution.py:226
  694.4 47.2 %reduce-scatter.23.cloned.1.call-done = bf16[768,768]{1,0:T(8,128)(2,1)} async-done(((bf16[3072,768]{1,0:T(8,128)(2,1)}), bf16[768,768]{1,0:T(8,128)(2,1)}) %reduce-scatter.23.cloned.1.call-update) | async-done | bytes 1179664 | tf_op jit(solution)/shard_map/reduce_scatter | solution.py:232
  741.6 50.3 %reduce-scatter.21.cloned.1.call-done = bf16[768,768]{1,0:T(8,128)(2,1)} async-done(((bf16[3072,768]{1,0:T(8,128)(2,1)}), bf16[768,768]{1,0:T(8,128)(2,1)}) %reduce-scatter.21.cloned.1.call-update) | async-done | bytes 1179664 | tf_op jit(solution)/shard_map/reduce_scatter | solution.py:232
  791.8 3.2 pad_maximum_fusion.2
  800.1 8.0 fusion.164
  821.5 11.3 %all-reduce.6 = (bf16[3072]{0:T(1024)(128)(2,1)}, bf16[3072]{0:T(1024)(128)(2,1)}) all-reduce(bf16[3072]{0:T(1024)(128)(2,1)} %get-tuple-element.443, bf16[3072]{0:T(1024)(128)(2,1)} %get-tuple-element.445), channel_id=15, replica_groups=mesh['dp'=8,'tensor'=4] {'tensor'}, use_global_device_ids=true, to_apply=%region_66.67.clone | all-reduce | flops 6144 | bytes 24576
  846.5 23.4 %all-reduce.4 = (bf16[2,2,192]{2,1,0:T(2,128)(2,1)S(1)}, bf16[2,768]{1,0:T(2,128)(2,1)S(1)}) all-reduce(bf16[2,2,192]{2,1,0:T(2,128)(2,1)S(1)} %pad_maximum_fusion.15, bf16[2,768]{1,0:T(2,128)(2,1)} %pad_maximum_fusion.14), channel_id=1, replica_groups=mesh['dp'=8,'tensor'=4] {'dp'}, use_global_device_ids=true, to_apply=%region_55.56 | all-reduce | flops 2304 | bytes 9216 | tf_op jit(solution)/shard_map/psum | solution.py:358
  872.7 4.3 scatter_custom_fusion.1
  877.2 41.6 %all-reduce.3 = (f32[768]{0:T(1024)}, f32[2,2,768]{2,1,0:T(2,128)}, f32[2,2,768]{2,1,0:T(2,128)}, f32[2,768]{1,0:T(2,128)}, f32[2,768]{1,0:T(2,128)}) all-reduce(f32[768]{0:T(1024)S(1)} %copy-done.82, f32[2,2,768]{2,1,0:T(2,128)S(1)} %pad_maximum_fusion.10, ...), channel_id=1, replica_groups=mesh['dp'=8,'tensor'=4] {'dp','tensor'}, use_global_device_ids=true, to_apply=%region_39.40 | all-reduce | flops 9984 | bytes 79872 | tf_op jit(solution)/shard_map/psum | solution.py:347
  918.8 147.8 %all-reduce.9.cloned.1.call-done = (bf16[2,3,768,192]{2,3,1,0:T(8,128)(2,1)}, bf16[2,192,768]{2,1,0:T(8,128)(2,1)}, bf16[2,768,768]{2,1,0:T(8,128)(2,1)}, bf16[2,768,768]{2,1,0:T(8,128)(2,1)}) async-done(((bf16[2,3,768,192]{2,3,1,0:T(8,128)(2,1)}, bf16[2,192,768]{2,1,0:T(8,128)(2,1)}, bf16[2,768,768]{2,1,0:T(8,128)(2,1)}, bf16[2,768,768]{2,1,0:T(8,128)(2,1)}), (bf16[2,3,768,192]{2,3,1,0:T(8,128)(2,1)}, ...) | async-done | bytes 7077904 | tf_op jit(solution)/shard_map/psum | solution.py:357
  1066.6 3.7 convert_element_type.429
  (503 shorter events, 205.3 us)
Async XLA Ops:
  7.2 15.1 %copy-start.71 = (bf16[2,2,768]{2,1,0:T(2,128)(2,1)S(1)}, bf16[2,2,768]{2,1,0:T(2,128)(2,1)}, u32[]{:S(2)}) copy-start(bf16[2,2,768]{2,1,0:T(2,128)(2,1)} %param.28) | copy-start | bytes 18436
  7.2 15.1 %copy-start.72 = (bf16[2,2,768]{2,1,0:T(2,128)(2,1)S(1)}, bf16[2,2,768]{2,1,0:T(2,128)(2,1)}, u32[]{:S(2)}) copy-start(bf16[2,2,768]{2,1,0:T(2,128)(2,1)} %param.27) | copy-start | bytes 18436
  7.2 39.3 %all-gather.15.cloned.1.call-start = ((), (), s32[]{:S(2)}) async-start(), calls=%async_computation.8 | async-start | bytes 2088960 | tf_op jit(solution)/shard_map/all_gather | solution.py:121
  8.0 15.4 %copy-start.5 = (s32[272]{0:T(512)}, s32[272]{0:T(512)S(1)}, u32[]{:S(2)}) copy-start(s32[272]{0:T(512)S(1)} %get-tuple-element.320) | copy-start | bytes 3268
  8.0 178.3 %copy-start.97 = (s32[272]{0:T(512)}, s32[272]{0:T(512)S(1)}, u32[]{:S(2)}) copy-start(s32[272]{0:T(512)S(1)} %get-tuple-element.321) | copy-start | bytes 3268
  8.0 15.5 %copy-start.92 = (bf16[2,2,192]{2,1,0:T(2,128)(2,1)S(1)}, bf16[2,2,192]{2,1,0:T(2,128)(2,1)}, u32[]{:S(2)}) copy-start(bf16[2,2,192]{2,1,0:T(2,128)(2,1)} %param.30) | copy-start | bytes 4612
  8.0 15.6 %copy-start.98 = (s32[4,6]{1,0:T(4,128)S(1)}, s32[4,6]{1,0:T(4,128)}, u32[]{:S(2)}) copy-start(s32[4,6]{1,0:T(4,128)} %param.24) | copy-start | bytes 292
  8.0 15.8 %copy-start.70 = (s32[4,272]{1,0:T(4,128)S(1)}, s32[4,272]{1,0:T(4,128)}, u32[]{:S(2)}) copy-start(s32[4,272]{1,0:T(4,128)} %param.25) | copy-start | bytes 13060
  21.8 80.7 %copy-start.7 = (bf16[272,768]{1,0:T(8,128)(2,1)}, bf16[272,768]{1,0:T(8,128)(2,1)S(1)}, u32[]{:S(2)}) copy-start(bf16[272,768]{1,0:T(8,128)(2,1)S(1)} %gather_fusion) | copy-start | bytes 1253380
  22.3 119.8 %copy-start.60 = (f32[768]{0:T(1024)}, f32[768]{0:T(1024)S(1)}, u32[]{:S(2)}) copy-start(f32[768]{0:T(1024)S(1)} %get-tuple-element.449) | copy-start | bytes 9220
  22.4 119.8 %copy-start.93 = (f32[768]{0:T(1024)}, f32[768]{0:T(1024)S(1)}, u32[]{:S(2)}) copy-start(f32[768]{0:T(1024)S(1)} %get-tuple-element.313) | copy-start | bytes 9220
  23.4 79.0 %reduce-scatter.9.cloned.1.call-start = ((), (), s32[]{:S(2)}) async-start(), calls=%async_computation.9 | async-start | bytes 4177920 | tf_op jit(solution)/shard_map/reduce_scatter | solution.py:135
  24.1 22.4 %copy-start.101 = (bf16[2,3,768,192]{2,3,1,0:T(8,128)(2,1)S(1)}, bf16[2,3,768,192]{2,3,1,0:T(8,128)(2,1)}, u32[]{:S(2)}) copy-start(bf16[2,3,768,192]{2,3,1,0:T(8,128)(2,1)} %param.29) | copy-start | bytes 5308420
  63.2 79.0 %all-gather.23.cloned.1.call-start = ((), (), s32[]{:S(2)}) async-start(), calls=%async_computation.20 | async-start | bytes 5898240 | tf_op jit(solution)/shard_map/all_gather | solution.py:193
  66.5 8.8 copy-start.90
  66.5 8.9 copy-start.85
  66.5 8.9 copy-start.86
  66.5 9.8 copy-start.9
  66.5 115.2 %all-gather.25.cloned.1.call-start = ((), (), s32[]{:S(2)}) async-start(), calls=%async_computation.21 | async-start | bytes 5898240 | tf_op jit(solution)/shard_map/all_gather | solution.py:195
  69.8 151.1 %all-gather.17.cloned.1.call-start = ((), (), s32[]{:S(2)}) async-start(), calls=%async_computation.10 | async-start | bytes 4177920 | tf_op jit(solution)/shard_map/all_gather | solution.py:121
  76.3 27.6 %copy-start.80 = (f32[272]{0:T(512)}, f32[272]{0:T(512)S(1)}, u32[]{:S(2)}) copy-start(f32[272]{0:T(512)S(1)} %convolution_reduce_fusion.1) | copy-start | bytes 3268
  76.3 110.0 %copy-start.68 = (f32[272]{0:T(512)}, f32[272]{0:T(512)S(1)}, u32[]{:S(2)}) copy-start(f32[272]{0:T(512)S(1)} %add_divide_fusion) | copy-start | bytes 3268
  103.8 44.5 %copy-start.13 = (f32[1,272,768]{2,1,0:T(8,128)}, f32[1,272,768]{2,1,0:T(8,128)S(1)}, u32[]{:S(2)}) copy-start(f32[1,272,768]{2,1,0:T(8,128)S(1)} %get-tuple-element.417) | copy-start | bytes 2506756
  103.8 44.4 %copy-start.66 = (f32[272]{0:T(512)}, f32[272]{0:T(512)S(1)}, u32[]{:S(2)}) copy-start(f32[272]{0:T(512)S(1)} %broadcast_multiply_fusion.10) | copy-start | bytes 3268
  104.1 44.2 %copy-start.75 = (f32[272]{0:T(512)}, f32[272]{0:T(512)S(1)}, u32[]{:S(2)}) copy-start(f32[272]{0:T(512)S(1)} %add_rsqrt_fusion.2) | copy-start | bytes 3268
  191.2 129.5 %reduce-scatter.11.cloned.1.call-start = ((), (), s32[]{:S(2)}) async-start(), calls=%async_computation.11 | async-start | bytes 8355840 | tf_op jit(solution)/shard_map/reduce_scatter | solution.py:135
  259.5 100.8 %all-gather.27.cloned.1.call-start = ((), (), s32[]{:S(2)}) async-start(), calls=%async_computation.22 | async-start | bytes 5898240 | tf_op jit(solution)/shard_map/all_gather | solution.py:193
  260.3 139.6 %all-gather.29.cloned.1.call-start = ((), (), s32[]{:S(2)}) async-start(), calls=%async_computation.23 | async-start | bytes 5898240 | tf_op jit(solution)/shard_map/all_gather | solution.py:195
  261.0 184.3 %all-gather.19.cloned.1.call-start = ((), (), s32[]{:S(2)}) async-start(), calls=%async_computation.12 | async-start | bytes 4177920 | tf_op jit(solution)/shard_map/all_gather | solution.py:156
  412.7 32.6 %copy-start.44 = (bf16[2,192,768]{2,1,0:T(8,128)(2,1)S(1)}, bf16[2,192,768]{2,1,0:T(8,128)(2,1)}, u32[]{:S(2)}) copy-start(bf16[2,192,768]{2,1,0:T(8,128)(2,1)} %param.31) | copy-start | bytes 1769476
  415.5 129.1 %reduce-scatter.13.cloned.1.call-start = ((), (), s32[]{:S(2)}) async-start(), calls=%async_computation.13 | async-start | bytes 4177920 | tf_op jit(solution)/shard_map/reduce_scatter | solution.py:176
  505.2 94.7 %all-gather.21.cloned.1.call-start = ((), (), s32[]{:S(2)}) async-start(), calls=%async_computation.14 | async-start | bytes 2088960 | tf_op jit(solution)/shard_map/all_gather | solution.py:156
  566.9 9.7 copy-start.78
  568.8 72.4 %reduce-scatter.19.cloned.1.call-start = ((), (), s32[]{:S(2)}) async-start(), calls=%async_computation.17 | async-start | bytes 5898240 | tf_op jit(solution)/shard_map/reduce_scatter | solution.py:226
  576.6 114.5 %reduce-scatter.17.cloned.1.call-start = ((), (), s32[]{:S(2)}) async-start(), calls=%async_computation.16 | async-start | bytes 5898240 | tf_op jit(solution)/shard_map/reduce_scatter | solution.py:226
  583.7 157.9 %reduce-scatter.23.cloned.1.call-start = ((), (), s32[]{:S(2)}) async-start(), calls=%async_computation.19 | async-start | bytes 5898240 | tf_op jit(solution)/shard_map/reduce_scatter | solution.py:232
  592.5 199.3 %reduce-scatter.21.cloned.1.call-start = ((), (), s32[]{:S(2)}) async-start(), calls=%async_computation.18 | async-start | bytes 5898240 | tf_op jit(solution)/shard_map/reduce_scatter | solution.py:232
  599.8 8.5 copy-start.1
  599.8 271.3 %reduce-scatter.15.cloned.1.call-start = ((), (), s32[]{:S(2)}) async-start(), calls=%async_computation.15 | async-start | bytes 2088960 | tf_op jit(solution)/shard_map/reduce_scatter | solution.py:176
  629.5 437.1 %all-reduce.9.cloned.1.call-start = ((), (), s32[]{:S(2)}) async-start(), calls=%async_computation.24 | async-start | bytes 14155776 | tf_op jit(solution)/shard_map/psum | solution.py:357
  800.1 15.6 %copy-start.81 = (f32[272]{0:T(512)S(1)}, f32[272]{0:T(512)}, u32[]{:S(2)}) copy-start(f32[272]{0:T(512)} %copy-done.80) | copy-start | bytes 3268
  800.1 38.8 %copy-start.8 = (bf16[272,768]{1,0:T(8,128)(2,1)S(1)}, bf16[272,768]{1,0:T(8,128)(2,1)}, u32[]{:S(2)}) copy-start(bf16[272,768]{1,0:T(8,128)(2,1)} %copy-done.7) | copy-start | bytes 1253380
  808.2 63.0 %copy-start.59 = (f32[768]{0:T(1024)S(1)}, f32[768]{0:T(1024)}, u32[]{:S(2)}) copy-start(f32[768]{0:T(1024)} %copy-done.58) | copy-start | bytes 9220
  808.2 63.0 %copy-start.63 = (f32[272]{0:T(512)S(1)}, f32[272]{0:T(512)}, u32[]{:S(2)}) copy-start(f32[272]{0:T(512)} %copy-done.62) | copy-start | bytes 3268
  808.2 63.0 %copy-start.65 = (f32[272]{0:T(512)S(1)}, f32[272]{0:T(512)}, u32[]{:S(2)}) copy-start(f32[272]{0:T(512)} %copy-done.64) | copy-start | bytes 3268
  808.2 64.6 %copy-start.16 = (f32[1,272,768]{2,1,0:T(8,128)S(1)}, f32[1,272,768]{2,1,0:T(8,128)}, u32[]{:S(2)}) copy-start(f32[1,272,768]{2,1,0:T(8,128)} %copy-done.13) | copy-start | bytes 2506756
  816.5 19.8 %copy-start.79 = (f32[272]{0:T(512)}, f32[272]{0:T(512)S(1)}, u32[]{:S(2)}) copy-start(f32[272]{0:T(512)S(1)} %subtract_multiply_fusion.2) | copy-start | bytes 3268
  877.1 193.2 %copy-start.4 = (f32[544,768]{1,0:T(8,128)}, f32[544,768]{1,0:T(8,128)S(1)}, u32[]{:S(2)}) copy-start(f32[544,768]{1,0:T(8,128)S(1)} %scatter_custom_fusion.1) | copy-start | bytes 5013508
  (85 other events, 292.4 us)
Sparse Core Ops, SparseCore 0:
  23.5 22.9 all-gather.14
  63.3 39.1 reduce-scatter.8
  104.7 37.4 all-gather.22
  144.2 37.4 all-gather.24
  191.3 29.6 all-gather.16
  259.6 60.9 reduce-scatter.10
  322.8 37.4 all-gather.26
  362.4 37.4 all-gather.28
  415.6 29.6 all-gather.18
  505.3 39.1 reduce-scatter.12
  568.9 20.2 all-gather.20
  592.3 47.8 reduce-scatter.18
  643.3 47.8 reduce-scatter.16
  693.7 47.8 reduce-scatter.22
  744.0 47.8 reduce-scatter.20
  795.0 28.7 reduce-scatter.14
  829.2 237.3 all-reduce.8
where the time goes:
time: 1090 us; the launch traced here: 1080 us
  waiting for transfers between devices  626 us (57%)
  matrix products  193 us (18%)
  blocking collectives  87.3 us (8%)
  other arithmetic  80 us (7%)
  local copies, waits for them, and re-layouts  77.8 us (7%)
  between operations  16.2 us (1%)
    psum x1, waiting for transfers between devices, body(): lax.psum(qkv_part.astype(jnp.bfloat16), 'dp').astype(jnp.float32)  148 us
    reduce_scatter x2, waiting for transfers between devices, dense_back(): lax.psum_scatter(second_part.astype(jnp.bfloat16), 'tensor', scatter_dime...  97.4 us
    reduce_scatter x2, waiting for transfers between devices, attention_forward(): lax.psum_scatter(jnp.einsum('gle,ed->gld', head_out, out_weights, preferr...  80 us
    all_gather x2, waiting for transfers between devices, dense_forward(): lax.all_gather(first_weights, 'tensor', axis=1, tiled=True)  74.4 us
    all_gather x2, waiting for transfers between devices, dense_forward(): lax.all_gather(second_weights, 'tensor', axis=0, tiled=True)  64.4 us
    reduce_scatter x2, waiting for transfers between devices, dense_back(): lax.psum_scatter(first_part.astype(jnp.bfloat16), 'tensor', scatter_dimen...  50 us
    all_gather x2, waiting for transfers between devices, attention_forward(): gathered = lax.all_gather(normed, 'tensor', axis=0, tiled=True)  42.2 us
    psum x1, blocking collectives, body(): lax.psum((router_part, gain_part, shift_part, out_bias_part, second_bias_...  41.6 us
  transfers between devices with their start and end apart: 17, of which 14 were waited for; matrix products, arithmetic and copies ran while one was open for 14% of the time, Pallas kernels for 0%

commit v1 on v0

v1 whole, which is shorter than its diff:
```python
import functools

import jax
import jax.numpy as jnp
from jax import lax
from jax.experimental import pallas as pl
from jax.experimental.pallas import tpu as pltpu
from jax.sharding import PartitionSpec as P

HEAD_DIM = 64
HID_TILE = 256

norm_eps = 1e-06
mask_fill = -1e30
half_root = 0.7071067811865476
inv_root_tau = 0.3989422804014327

F32 = jnp.float32
BF16 = jnp.bfloat16
NN = (((1,), (0,)), ((), ()))
NT = (((1,), (1,)), ((), ()))
TN = (((0,), (0,)), ((), ()))


def mm(a, b, dims):
    return lax.dot_general(a, b, dims, preferred_element_type=F32)


def norm_parts(rows):
    centred = rows - jnp.mean(rows, axis=-1, keepdims=True)
    inv_std = lax.rsqrt(jnp.mean(centred * centred, axis=-1, keepdims=True) + norm_eps)
    return centred * inv_std, inv_std


class Blocks:
    def __init__(self, layer, sources, buffers, sems, order):
        self.layer, self.sources, self.buffers = layer, sources, buffers
        self.sems, self.order = sems, order

    def copies(self, block, slot):
        found = []
        for part, (own, got) in enumerate(self.sources):
            src = own.at[self.layer] if block == 0 else got.at[block - 1]
            found.append(
                pltpu.make_async_copy(src, self.buffers[part].at[slot], self.sems.at[slot, part])
            )
        return found

    def begin(self, step, slot):
        for place, block in enumerate(self.order):

            @pl.when(step == place)
            def _():
                for copy in self.copies(block, slot):
                    copy.start()

    def turn(self, step):
        slot = lax.rem(step, 2)

        @pl.when(step == 0)
        def _():
            self.begin(step, slot)

        @pl.when(step + 1 < len(self.order))
        def _():
            self.begin(step + 1, 1 - slot)

        for place, block in enumerate(self.order):

            @pl.when(step == place)
            def _():
                for copy in self.copies(block, slot):
                    copy.wait()

        return slot


def pairs(refs):
    return [(refs[i], refs[i + 1]) for i in range(0, len(refs), 2)]


any_spec = pl.BlockSpec(memory_space=pl.ANY)


def whole(shape):
    return pl.BlockSpec(shape, lambda s: (0,) * len(shape))


def params():
    return pltpu.CompilerParams(
        dimension_semantics=("arbitrary",), vmem_limit_bytes=60 * 1024 * 1024
    )


def attention_forward_kernel(layer, order, *refs):
    (u_ref, gain_ref, shift_ref, crop_col, crop_row, q_bias, v_bias, out_bias) = refs[:8]
    sources = pairs(refs[8:10])
    (res_ref, q_ref, k_ref, v_ref, ho_ref, normed, acc, wbuf, sems) = refs[10:]
    step = pl.program_id(0)
    blocks = Blocks(layer, sources, [wbuf], sems, order)

    @pl.when(step == 0)
    def _():
        xhat, _ = norm_parts(u_ref[...].astype(F32))
        normed[...] = (xhat * gain_ref[...] + shift_ref[...]).astype(BF16)
        acc[...] = u_ref[...].astype(F32) + out_bias[...]

    slot = blocks.turn(step)
    width = wbuf.shape[1] // 4
    rows = normed[...]
    scale = HEAD_DIM**-0.5
    q = (mm(rows, wbuf[slot, 0:width], NT) + q_bias[0]).astype(BF16) * BF16(scale)
    k = mm(rows, wbuf[slot, width : 2 * width], NT).astype(BF16)
    v = (mm(rows, wbuf[slot, 2 * width : 3 * width], NT) + v_bias[0]).astype(BF16)
    q_ref[0] = q
    k_ref[0] = k
    v_ref[0] = v
    length = q.shape[0]
    tile = length // 2 if length > 320 else length
    for head in range(width // HEAD_DIM):
        lanes = slice(head * HEAD_DIM, (head + 1) * HEAD_DIM)
        keys, vals = k_ref[0, :, lanes], v_ref[0, :, lanes]
        for part in range(length // tile):
            own = slice(part * tile, (part + 1) * tile)
            scores = mm(q_ref[0, own, lanes], keys, NT)
            scores = jnp.where(crop_col[own] == crop_row[...], scores, mask_fill)
            top = jnp.max(scores, axis=-1, keepdims=True)
            weight = jnp.exp(scores - top)
            total = jnp.sum(weight, axis=-1, keepdims=True)
            head_out = mm(weight.astype(BF16), vals, NN) / total
            ho_ref[0, own, lanes] = head_out.astype(BF16)
    acc[...] += mm(ho_ref[0], wbuf[slot, 3 * width : 4 * width], NN)

    @pl.when(step == len(order) - 1)
    def _():
        res_ref[...] = acc[...]


def attention_forward(u, gain, shift, crops, biases, out_bias, layer, weights, order):
    length, features = u.shape
    width = biases[0].shape[-1]

    def of_block(s):
        return (s if order[0] == 0 else order[0] - s, 0, 0)

    saved = jax.ShapeDtypeStruct((len(order), length, width), BF16)
    kernel = functools.partial(attention_forward_kernel, layer, tuple(order))

    flops = 2 * length * features * 4 * width * len(order) + 4 * length * length * width * len(
        order
    )
    return pl.pallas_call(
        kernel,
        out_shape=[jax.ShapeDtypeStruct((length, features), F32)] + [saved] * 4,
        grid_spec=pl.GridSpec(
            grid=(len(order),),
            in_specs=[
                whole((length, features)),
                whole((1, features)),
                whole((1, features)),
                whole((length, 1)),
                whole((1, length)),
                pl.BlockSpec((1, 1, width), of_block),
                pl.BlockSpec((1, 1, width), of_block),
                whole((1, features)),
            ]
            + [any_spec] * len(weights),
            out_specs=[whole((length, features))]
            + [pl.BlockSpec((1, length, width), of_block)] * 4,
            scratch_shapes=[
                pltpu.VMEM((length, features), BF16),
                pltpu.VMEM((length, features), F32),
                pltpu.VMEM((2, 4 * width, features), BF16),
                pltpu.SemaphoreType.DMA((2, 1)),
            ],
        ),
        compiler_params=params(),
        name="attention_forward",
        cost_estimate=pl.CostEstimate(
            flops=flops,
            transcendentals=length * length * len(order) * width // HEAD_DIM,
            bytes_accessed=length * features * 16 + 8 * width * features * len(order),
        ),
    )(u, gain, shift, crops[0], crops[1], biases[0], biases[1], out_bias, *weights)


class Results:
    def __init__(self, targets, staging, sems, order):
        self.targets, self.staging, self.sems, self.order = targets, staging, sems, order

    def copies(self, place, slot):
        return [
            pltpu.make_async_copy(
                self.staging[i].at[slot], target.at[self.order[place]], self.sems.at[slot, i]
            )
            for i, target in enumerate(self.targets)
        ]

    def ready(self, step):
        for place in range(len(self.order)):

            @pl.when(step == place + 2)
            def _():
                for copy in self.copies(place, place % 2):
                    copy.wait()

    def send(self, step):
        count = len(self.order)
        for place in range(count):

            @pl.when(step == place)
            def _():
                for copy in self.copies(place, place % 2):
                    copy.start()

        @pl.when(step == count - 1)
        def _():
            for place in range(max(0, count - 2), count):
                for copy in self.copies(place, place % 2):
                    copy.wait()


def norm_back_into(g_normed, u, gain, base, res_ref, gain_ref, shift_ref):
    xhat, inv_std = norm_parts(u)
    scaled = g_normed * gain
    inner = jnp.mean(scaled, axis=-1, keepdims=True) + xhat * jnp.mean(
        scaled * xhat, axis=-1, keepdims=True
    )
    res_ref[...] = base + inv_std * (scaled - inner)
    gain_ref[...] = jnp.sum(g_normed * xhat, axis=0, keepdims=True)
    shift_ref[...] = jnp.sum(g_normed, axis=0, keepdims=True)


def attention_backward_kernel(layer, order, *refs):
    (g_ref, u_ref, gain_ref, shift_ref, crop_col, crop_row, q_ref, k_ref, v_ref, ho_ref) = refs[
        :10
    ]
    sources = pairs(refs[10:12])
    refs = refs[12:]
    count = len(order)
    res_ref, gain_out, shift_out, bias_out, qb_out, vb_out = refs[:6]
    targets = [refs[6]]
    normed, grad_low, acc, back, wbuf, staging, sems, out_sems = refs[7:]
    step = pl.program_id(0)
    blocks = Blocks(layer, sources, [wbuf], sems, order)
    results = Results(targets, [staging], out_sems, order)

    @pl.when(step == 0)
    def _():
        xhat, _ = norm_parts(u_ref[...].astype(F32))
        normed[...] = (xhat * gain_ref[...] + shift_ref[...]).astype(BF16)
        low = g_ref[...].astype(BF16)
        grad_low[...] = low
        bias_out[...] = jnp.sum(low.astype(F32), axis=0, keepdims=True)
        acc[...] = jnp.zeros_like(acc)

    slot = blocks.turn(step)
    results.ready(step)
    width = wbuf.shape[1] // 4
    low = grad_low[...]
    head_grads = mm(low, wbuf[slot, 3 * width : 4 * width], NT).astype(BF16)
    staging[slot, 3 * width : 4 * width] = mm(ho_ref[0], low, TN).astype(BF16)
    scale = HEAD_DIM**-0.5
    for head in range(width // HEAD_DIM):
        lanes = slice(head * HEAD_DIM, (head + 1) * HEAD_DIM)
        q, k, v = q_ref[0, :, lanes], k_ref[0, :, lanes], v_ref[0, :, lanes]
        gh = head_grads[:, lanes]
        scores = mm(k, q, NT)
        scores = jnp.where(crop_col[...] == crop_row[...], scores, mask_fill)
        top = jnp.max(scores, axis=0, keepdims=True)
        weight = jnp.exp(scores - top)
        probs = weight * (1.0 / jnp.sum(weight, axis=0, keepdims=True))
        prob_grad = mm(v, gh, NT)
        inner = jnp.sum(probs * prob_grad, axis=0, keepdims=True)
        score_grad = (probs * (prob_grad - inner)).astype(BF16)
        back[2, :, lanes] = mm(probs.astype(BF16), gh, NN).astype(BF16)
        back[1, :, lanes] = mm(score_grad, q, NN).astype(BF16)
        back[0, :, lanes] = (mm(score_grad, k, TN) * scale).astype(BF16)
    qb_out[0] = jnp.sum(back[0].astype(F32), axis=0, keepdims=True)
    vb_out[0] = jnp.sum(back[2].astype(F32), axis=0, keepdims=True)
    rows = normed[...]
    for part in range(3):
        own = slice(part * width, (part + 1) * width)
        staging[slot, own] = mm(back[part], rows, TN).astype(BF16)
        acc[...] += mm(back[part], wbuf[slot, own], NN)
    results.send(step)

    @pl.when(step == count - 1)
    def _():
        norm_back_into(
            acc[...], u_ref[...].astype(F32), gain_ref[...], g_ref[...], res_ref, gain_out, shift_out
        )


def attention_backward(g, u, gain, shift, crops, saved, layer, weights, order):
    length, features = g.shape
    width = saved[0].shape[-1]
    count = len(order)

    def of_block(s):
        return (s if order[0] == 0 else order[0] - s, 0, 0)

    kernel = functools.partial(attention_backward_kernel, layer, tuple(order))

    row = jax.ShapeDtypeStruct((1, features), F32)
    bias = jax.ShapeDtypeStruct((count, 1, width), F32)
    flops = 2 * length * features * 8 * width * count + 10 * length * length * width * count
    return pl.pallas_call(
        kernel,
        out_shape=[jax.ShapeDtypeStruct((length, features), F32), row, row, row, bias, bias]
        + [jax.ShapeDtypeStruct((count, 4 * width, features), BF16)],
        grid_spec=pl.GridSpec(
            grid=(count,),
            in_specs=[
                whole((length, features)),
                whole((length, features)),
                whole((1, features)),
                whole((1, features)),
                whole((length, 1)),
                whole((1, length)),
            ]
            + [pl.BlockSpec((1, length, width), of_block)] * 4
            + [any_spec] * len(weights),
            out_specs=[whole((length, features))]
            + [whole((1, features))] * 3
            + [pl.BlockSpec((1, 1, width), of_block)] * 2
            + [any_spec],
            scratch_shapes=[
                pltpu.VMEM((length, features), BF16),
                pltpu.VMEM((length, features), BF16),
                pltpu.VMEM((length, features), F32),
                pltpu.VMEM((3, length, width), BF16),
                pltpu.VMEM((2, 4 * width, features), BF16),
                pltpu.VMEM((2, 4 * width, features), BF16),
                pltpu.SemaphoreType.DMA((2, 1)),
                pltpu.SemaphoreType.DMA((2, 1)),
            ],
        ),
        compiler_params=params(),
        name="attention_backward",
        cost_estimate=pl.CostEstimate(
            flops=flops,
            transcendentals=length * length * count * width // HEAD_DIM,
            bytes_accessed=length * features * 20 + 16 * width * features * count,
        ),
    )(g, u, gain, shift, crops[0], crops[1], *saved, *weights)


def ffn_forward_kernel(layer, order, *refs):
    (u_ref, gain_ref, shift_ref, b1_ref, b2_ref) = refs[:5]
    sources = pairs(refs[5:9])
    res_ref, normed, acc, w1, w2, sems = refs[9:]
    step = pl.program_id(0)
    blocks = Blocks(layer, sources, [w1, w2], sems, order)

    @pl.when(step == 0)
    def _():
        xhat, _ = norm_parts(u_ref[...].astype(F32))
        normed[...] = (xhat * gain_ref[...] + shift_ref[...]).astype(BF16)
        acc[...] = u_ref[...].astype(F32) + b2_ref[...]

    slot = blocks.turn(step)

    def tile(t, carry):
        cols = pl.ds(pl.multiple_of(t * HID_TILE, HID_TILE), HID_TILE)
        preact = mm(normed[...], w1[slot, :, cols], NN) + b1_ref[0, :, cols]
        hidden = (0.5 * preact * (1.0 + lax.erf(preact * half_root))).astype(BF16)
        acc[...] += mm(hidden, w2[slot, cols, :], NN)
        return carry

    lax.fori_loop(0, w1.shape[2] // HID_TILE, tile, 0)

    @pl.when(step == len(order) - 1)
    def _():
        res_ref[...] = acc[...]


def ffn_forward(u, gain, shift, b1, b2, layer, weights, order):
    length, features = u.shape
    hidden = b1.shape[-1]

    def of_block(s):
        return (s if order[0] == 0 else order[0] - s, 0, 0)

    kernel = functools.partial(ffn_forward_kernel, layer, tuple(order))

    return pl.pallas_call(
        kernel,
        out_shape=jax.ShapeDtypeStruct((length, features), F32),
        grid_spec=pl.GridSpec(
            grid=(len(order),),
            in_specs=[
                whole((length, features)),
                whole((1, features)),
                whole((1, features)),
                pl.BlockSpec((1, 1, hidden), of_block),
                whole((1, features)),
            ]
            + [any_spec] * len(weights),
            out_specs=whole((length, features)),
            scratch_shapes=[
                pltpu.VMEM((length, features), BF16),
                pltpu.VMEM((length, features), F32),
                pltpu.VMEM((2, features, hidden), BF16),
                pltpu.VMEM((2, hidden, features), BF16),
                pltpu.SemaphoreType.DMA((2, 2)),
            ],
        ),
        compiler_params=params(),
        name="ffn_forward",
        cost_estimate=pl.CostEstimate(
            flops=4 * length * features * hidden * len(order),
            transcendentals=length * hidden * len(order),
            bytes_accessed=length * features * 8 + 4 * hidden * features * len(order),
        ),
    )(u, gain, shift, b1, b2, *weights)


def ffn_both_kernel(layer, order, forward, *refs):
    (u_ref, g_ref, gain_ref, shift_ref, b1_ref, b2_ref) = refs[:6]
    sources = pairs(refs[6:10])
    refs = refs[10:]
    count = len(order)
    res_ref, gain_out, shift_out, b2_out, b1_out = refs[:5]
    refs = refs[5:]
    if forward:
        out_ref, refs = refs[0], refs[1:]
    targets = refs[:2]
    refs = refs[2:]
    normed, grad_low, acc_back, w1, w2, st1, st2, sems, out_sems = refs[:9]
    acc = refs[9] if forward else None
    step = pl.program_id(0)
    blocks = Blocks(layer, sources, [w1, w2], sems, order)
    results = Results(targets, [st1, st2], out_sems, order)

    @pl.when(step == 0)
    def _():
        xhat, _ = norm_parts(u_ref[...].astype(F32))
        normed[...] = (xhat * gain_ref[...] + shift_ref[...]).astype(BF16)
        low = g_ref[...].astype(BF16)
        grad_low[...] = low
        b2_out[...] = jnp.sum(low.astype(F32), axis=0, keepdims=True)
        acc_back[...] = jnp.zeros_like(acc_back)
        if forward:
            acc[...] = u_ref[...].astype(F32) + b2_ref[...]

    slot = blocks.turn(step)
    results.ready(step)

    def tile(t, carry):
        cols = pl.ds(pl.multiple_of(t * HID_TILE, HID_TILE), HID_TILE)
        rows, low = normed[...], grad_low[...]
        preact = mm(rows, w1[slot, :, cols], NN) + b1_ref[0, :, cols]
        half = 0.5 * (1.0 + lax.erf(preact * half_root))
        hidden = (preact * half).astype(BF16)
        slope = half + preact * (inv_root_tau * jnp.exp(-0.5 * preact * preact))
        if forward:
            acc[...] += mm(hidden, w2[slot, cols, :], NN)
        st2[slot, cols, :] = mm(hidden, low, TN).astype(BF16)
        pre_grad = (mm(low, w2[slot, cols, :], NT) * slope).astype(BF16)
        b1_out[0, :, cols] = jnp.sum(pre_grad.astype(F32), axis=0, keepdims=True)
        st1[slot, :, cols] = mm(rows, pre_grad, TN).astype(BF16)
        acc_back[...] += mm(pre_grad, w1[slot, :, cols], NT)
        return carry

    lax.fori_loop(0, w1.shape[2] // HID_TILE, tile, 0)
    results.send(step)

    @pl.when(step == count - 1)
    def _():
        if forward:
            out_ref[...] = acc[...].astype(BF16)
        norm_back_into(
            acc_back[...],
            u_ref[...].astype(F32),
            gain_ref[...],
            g_ref[...].astype(F32),
            res_ref,
            gain_out,
            shift_out,
        )


def ffn_both(u, g, gain, shift, b1, b2, layer, weights, order, forward):
    length, features = u.shape
    hidden = b1.shape[-1]
    count = len(order)

    def of_block(s):
        return (s if order[0] == 0 else order[0] - s, 0, 0)

    kernel = functools.partial(ffn_both_kernel, layer, tuple(order), forward)

    row = jax.ShapeDtypeStruct((1, features), F32)
    out_shape = [
        jax.ShapeDtypeStruct((length, features), F32),
        row,
        row,
        row,
        jax.ShapeDtypeStruct((count, 1, hidden), F32),
    ]
    out_specs = [whole((length, features))] + [whole((1, features))] * 3
    out_specs += [pl.BlockSpec((1, 1, hidden), of_block)]
    scratch = [
        pltpu.VMEM((length, features), BF16),
        pltpu.VMEM((length, features), BF16),
        pltpu.VMEM((length, features), F32),
        pltpu.VMEM((2, features, hidden), BF16),
        pltpu.VMEM((2, hidden, features), BF16),
        pltpu.VMEM((2, features, hidden), BF16),
        pltpu.VMEM((2, hidden, features), BF16),
        pltpu.SemaphoreType.DMA((2, 2)),
        pltpu.SemaphoreType.DMA((2, 2)),
    ]
    if forward:
        out_shape += [jax.ShapeDtypeStruct((length, features), BF16)]
        out_specs += [whole((length, features))]
        scratch += [pltpu.VMEM((length, features), F32)]
    out_shape += [jax.ShapeDtypeStruct((count, features, hidden), BF16)]
    out_shape += [jax.ShapeDtypeStruct((count, hidden, features), BF16)]
    out_specs += [any_spec] * 2
    return pl.pallas_call(
        kernel,
        out_shape=out_shape,
        grid_spec=pl.GridSpec(
            grid=(count,),
            in_specs=[
                whole((length, features)),
                whole((length, features)),
                whole((1, features)),
                whole((1, features)),
                pl.BlockSpec((1, 1, hidden), of_block),
                whole((1, features)),
            ]
            + [any_spec] * len(weights),
            out_specs=out_specs,
            scratch_shapes=scratch,
        ),
        compiler_params=params(),
        name="ffn_both" if forward else "ffn_backward",
        cost_estimate=pl.CostEstimate(
            flops=(12 if forward else 10) * length * features * hidden * count,
            transcendentals=2 * length * hidden * count,
            bytes_accessed=length * features * 12 + 8 * hidden * features * count,
        ),
    )(u, g, gain, shift, b1, b2, *weights)


MESH = pl.DeviceIdType.MESH


class Place:
    def __init__(self, n_data):
        self.data, self.tensor = lax.axis_index("dp"), lax.axis_index("tensor")
        self.bits = [1 << b for b in range(n_data.bit_length() - 1)]
        self.sides = [lax.rem(self.data // bit, 2) for bit in self.bits]

    def by_tensor(self, bit):
        own = lax.rem(self.tensor // bit, 2)
        return (self.data, self.tensor + bit * (1 - 2 * own))

    def by_data(self, number):
        bit = self.bits[number]
        return (self.data + bit * (1 - 2 * self.sides[number]), self.tensor)


def greet(partners):
    barrier = pltpu.get_barrier_semaphore()
    for partner in partners:
        pl.semaphore_signal(barrier, inc=1, device_id=partner, device_id_type=MESH)
    pl.semaphore_wait(barrier, len(partners))


def remote(src, dst, send_sem, recv_sem, device):
    return pltpu.make_async_remote_copy(
        src_ref=src,
        dst_ref=dst,
        send_sem=send_sem,
        recv_sem=recv_sem,
        device_id=device,
        device_id_type=MESH,
    )


KINDS = ("near", "y", "z", "x", "core_y", "core_z", "core_x")


def gather_kernel(n_data, units, attn, fc1, fc2, small, *refs):
    outs, small_out = refs[: len(units)], refs[len(units)]
    send_sems, recv_sems, small_send, small_recv, local_sem = refs[len(units) + 1 :]
    place = Place(n_data)
    core, across = place.by_tensor(1), place.by_tensor(2)
    side_x, side_z = place.by_data(0), place.by_data(1)
    x, z = place.sides[0], place.sides[1]
    third = outs[0].shape[1] // 3
    by_y = x * (1 - z) + 2 * z
    by_z = 2 * (1 - z) + x * z
    by_x = 1 - x
    source = {"attn": attn, "fc1": fc1, "fc2": fc2}

    def rows(index):
        return pl.ds(pl.multiple_of(index * third, third), third)

    def own(u):
        return source[units[u][0]].at[units[u][1]]

    def copy(u, kind):
        number = KINDS.index(kind)
        sems = (send_sems.at[u, number], recv_sems.at[u, number])
        got = outs[u]
        if kind == "near":
            return remote(own(u), got.at[0], *sems, core)
        if kind == "y":
            return remote(own(u).at[rows(by_y)], got.at[1, rows(by_y)], *sems, across)
        if kind == "z":
            return remote(got.at[1, rows(by_y)], got.at[1, rows(by_y)], *sems, side_z)
        if kind == "x":
            return remote(got.at[1, rows(x)], got.at[1, rows(x)], *sems, side_x)
        index = {"core_y": by_y, "core_z": by_z, "core_x": by_x}[kind]
        return remote(got.at[1, rows(index)], got.at[2, rows(index)], *sems, core)

    greet([core, across, side_x, side_z])
    little = [
        pltpu.make_async_copy(small, small_out.at[0], local_sem),
        remote(small, small_out.at[1], small_send.at[0], small_recv.at[0], core),
        remote(small, small_out.at[2], small_send.at[1], small_recv.at[1], across),
        remote(small_out.at[2], small_out.at[3], small_send.at[2], small_recv.at[2], core),
    ]
    for item in little[:3]:
        item.start()
    count = len(units)
    copy(0, "y").start()
    copy(1, "y").start()
    copy(0, "near").start()
    for turn in range(count + 2):
        u = turn
        if u < count:
            copy(u, "y").wait_recv()
            if u + 2 < count:
                copy(u + 2, "y").start()
            copy(u, "z").start()

            @pl.when(z == 0)
            def _():
                copy(u, "x").start()

            copy(u, "core_y").start()
            if u + 1 < count:
                copy(u + 1, "near").start()
        u = turn - 1
        if 0 <= u < count:
            copy(u, "z").wait_recv()

            @pl.when(z == 1)
            def _():
                copy(u, "x").start()

            copy(u, "core_z").start()
        u = turn - 2
        if 0 <= u < count:
            copy(u, "x").wait_recv()
            copy(u, "core_x").start()
        if turn == 0:
            little[2].wait_recv()
            little[3].start()
    little[0].wait()
    for item in little[1:]:
        item.wait_send()
    little[1].wait_recv()
    little[3].wait_recv()
    for u in range(count):
        for kind in KINDS:
            copy(u, kind).wait_send()
            if kind not in ("y", "z", "x"):
                copy(u, kind).wait_recv()


def gather_weights(attn, fc1, fc2, small):
    n_data, group = lax.axis_size("dp"), lax.axis_size("tensor")
    units = [(kind, layer) for layer in range(2) for kind in ("attn", "fc1", "fc2")]
    kinds = {"attn": attn, "fc1": fc1, "fc2": fc2}
    out = pl.pallas_call(
        functools.partial(gather_kernel, n_data, units),
        out_shape=[
            jax.ShapeDtypeStruct((group - 1,) + kinds[kind].shape[1:], BF16) for kind, _ in units
        ]
        + [jax.ShapeDtypeStruct((group,) + small.shape, small.dtype)],
        in_specs=[any_spec] * 4,
        out_specs=[any_spec] * (len(units) + 1),
        scratch_shapes=[
            pltpu.SemaphoreType.DMA((len(units), len(KINDS))),
            pltpu.SemaphoreType.DMA((len(units), len(KINDS))),
            pltpu.SemaphoreType.DMA((3,)),
            pltpu.SemaphoreType.DMA((3,)),
            pltpu.SemaphoreType.DMA,
        ],
        compiler_params=pltpu.CompilerParams(collective_id=1, has_side_effects=True),
        name="gather_weights",
    )(attn, fc1, fc2, small)
    return {unit: got for unit, got in zip(units, out)}, out[-1]


def split_in_two(region, side):
    row, n_rows, lane, n_lanes = region
    if n_rows >= 32:
        half = n_rows // 2
        keep = (pl.multiple_of(row + side * half, half), half, lane, n_lanes)
        give = (pl.multiple_of(row + (1 - side) * half, half), half, lane, n_lanes)
    else:
        half = n_lanes // 2
        keep = (row, n_rows, pl.multiple_of(lane + side * half, half), half)
        give = (row, n_rows, pl.multiple_of(lane + (1 - side) * half, half), half)
    return keep, give


def view(ref, chunk, region):
    row, n_rows, lane, n_lanes = region
    return ref.at[chunk, pl.ds(row, n_rows), pl.ds(lane, n_lanes)]


def reduce_kernel(n_data, n_units, chunk_rows, *refs):
    units, little_in = refs[:n_units], refs[n_units]
    outs, little_out = refs[n_units + 1 : 2 * n_units + 1], refs[2 * n_units + 1]
    refs = refs[2 * n_units + 2 :]
    own, far, got_own, got_far, got_y, total = refs[:6]
    place = Place(n_data)
    n_bits = len(place.bits)
    got_bits = refs[6 : 6 + n_bits]
    little, little_got, sends, recvs, loads, stores, little_send, little_recv = refs[6 + n_bits :]
    per_unit = units[0].shape[1] // chunk_rows
    count = n_units * per_unit
    lanes = units[0].shape[2]
    core, across = place.by_tensor(1), place.by_tensor(2)
    partners = [place.by_data(i) for i in range(n_bits)]

    keeps, gives = [], []
    region = (0, chunk_rows, 0, lanes)
    for i in range(n_bits):
        region, give = split_in_two(region, place.sides[i])
        keeps.append(region)
        gives.append(give)
    wholes = [(0, chunk_rows, 0, lanes)] + keeps

    def add(dst, a, b):
        dst[...] = (a[...].astype(F32) + b[...].astype(F32)).astype(BF16)

    def rows_of(chunk):
        return pl.ds(pl.multiple_of(lax.rem(chunk, per_unit) * chunk_rows, chunk_rows), chunk_rows)

    def core_copies(unit, c):
        rows = rows_of(c)
        return [
            remote(unit.at[3, rows], got_far.at[c], sends.at[0, c], recvs.at[0, c], core),
            remote(unit.at[1, rows], got_own.at[c], sends.at[1, c], recvs.at[1, c], core),
        ]

    def load_copies(unit, c):
        rows = rows_of(c)
        return [
            pltpu.make_async_copy(unit.at[2, rows], far.at[c], loads.at[0, c]),
            pltpu.make_async_copy(unit.at[0, rows], own.at[c], loads.at[1, c]),
        ]

    def y_copy(c):
        return remote(far.at[c], got_y.at[c], sends.at[2, c], recvs.at[2, c], across)

    def halve_copy(i, c):
        row, n_rows, lane, n_lanes = gives[i]
        return remote(
            view(own, c, gives[i]), got_bits[i].at[c], sends.at[3 + i, c], recvs.at[3 + i, c],
            partners[i],
        )

    def double_copy(i, c):
        number = 3 + n_bits + i
        piece = view(total, c, keeps[i])
        return remote(piece, piece, sends.at[number, c], recvs.at[number, c], partners[i])

    def store_copy(unit_out, c):
        return pltpu.make_async_copy(total.at[c], unit_out.at[rows_of(c)], stores.at[c])

    def per_unit_do(c, act):
        for number in range(n_units):

            @pl.when(c // per_unit == number)
            def _():
                act(number)

    def stage_load(c):
        def act(number):
            for item in core_copies(units[number], c) + load_copies(units[number], c):
                item.start()

        per_unit_do(c, act)

    def stage_core(c):
        core_pair, load_pair = core_copies(units[0], c), load_copies(units[0], c)
        load_pair[0].wait()
        core_pair[0].wait_recv()
        add(far.at[c], far.at[c], got_far.at[c])
        y_copy(c).start()
        load_pair[1].wait()
        core_pair[1].wait_recv()
        add(own.at[c], own.at[c], got_own.at[c])

    def stage_y(c):
        y_copy(c).wait_recv()
        add(own.at[c], own.at[c], got_y.at[c])
        halve_copy(0, c).start()

    def stage_halve(i):
        def run(c):
            halve_copy(i, c).wait_recv()
            kept = view(own, c, keeps[i])
            if i + 1 < n_bits:
                add(kept, kept, got_bits[i].at[c])
                halve_copy(i + 1, c).start()
            else:
                add(view(total, c, keeps[i]), kept, got_bits[i].at[c])
                double_copy(i, c).start()

        return run

    def stage_double(i):
        def run(c):
            double_copy(i, c).wait_recv()
            if i > 0:
                double_copy(i - 1, c).start()
            else:
                per_unit_do(c, lambda number: store_copy(outs[number], c).start())

        return run

    stages = [stage_load, stage_core, stage_y]
    stages += [stage_halve(i) for i in range(n_bits)]
    stages += [stage_double(i) for i in reversed(range(n_bits))]

    ways = partners + [core, across]
    head = little_in.shape[0] - 8 * 4

    def little_copy(i):
        return remote(
            little.at[i], little_got.at[i], little_send.at[i], little_recv.at[i], ways[i]
        )

    def little_turn(i):
        if i > 0:
            little_copy(i - 1).wait_recv()
            bit = 0 if i - 1 < n_bits else 1 << (i - 1 - n_bits)
            if bit == 0:
                little[i] = little[i - 1] + little_got[i - 1]
            else:
                little[i, 0:head] = little[i - 1, 0:head] + little_got[i - 1, 0:head]
                for block in range(4):
                    at = slice(head + 8 * block, head + 8 * block + 8)
                    there = slice(head + 8 * (block ^ bit), head + 8 * (block ^ bit) + 8)
                    little[i, at] = little[i - 1, at] + little_got[i - 1, there]
        else:
            little[0] = little_in[...]
        if i < len(ways):
            little_copy(i).start()
        else:
            little_out[...] = little[i]

    greet([core, across] + partners)

    def turn(t, carry):
        for number, stage in enumerate(stages):
            c = t - number

            @pl.when(jnp.logical_and(c >= 0, c < count))
            def _():
                stage(c)

        for i in range(len(ways) + 1):

            @pl.when(t == i + 1)
            def _():
                little_turn(i)

        return carry

    lax.fori_loop(0, count + len(stages) - 1, turn, 0)

    def finish(c, carry):
        for item in core_copies(units[0], c):
            item.wait_send()
        y_copy(c).wait_send()
        for i in range(n_bits):
            halve_copy(i, c).wait_send()
            double_copy(i, c).wait_send()
        store_copy(outs[0], c).wait()
        return carry

    lax.fori_loop(0, count, finish, 0)
    for i in range(len(ways)):
        little_copy(i).wait_send()


def reduce_gradients(units, little):
    n_data = lax.axis_size("dp")
    n_bits = n_data.bit_length() - 1
    rows, lanes = units[0].shape[1:]
    chunk_rows = rows // 3
    count = 3 * len(units)
    n_ways = n_bits + 2
    pieces, region = [], (chunk_rows, lanes)
    for _ in range(n_bits):
        row, lane = region
        region = (row // 2, lane) if row >= 32 else (row, lane // 2)
        pieces.append(region)
    chunk = pltpu.VMEM((count, chunk_rows, lanes), BF16)
    vmem = pl.BlockSpec(memory_space=pltpu.VMEM)
    out = pl.pallas_call(
        functools.partial(reduce_kernel, n_data, len(units), chunk_rows),
        out_shape=[jax.ShapeDtypeStruct((rows, lanes), BF16)] * len(units)
        + [jax.ShapeDtypeStruct(little.shape, F32)],
        in_specs=[any_spec] * len(units) + [vmem],
        out_specs=[any_spec] * len(units) + [vmem],
        scratch_shapes=[chunk] * 6
        + [pltpu.VMEM((count,) + piece, BF16) for piece in pieces]
        + [
            pltpu.VMEM((n_ways + 1,) + little.shape, F32),
            pltpu.VMEM((n_ways,) + little.shape, F32),
            pltpu.SemaphoreType.DMA((3 + 2 * n_bits, count)),
            pltpu.SemaphoreType.DMA((3 + 2 * n_bits, count)),
            pltpu.SemaphoreType.DMA((2, count)),
            pltpu.SemaphoreType.DMA((count,)),
            pltpu.SemaphoreType.DMA((n_ways,)),
            pltpu.SemaphoreType.DMA((n_ways,)),
        ],
        compiler_params=pltpu.CompilerParams(
            collective_id=2, has_side_effects=True, vmem_limit_bytes=60 * 1024 * 1024
        ),
        name="reduce_gradients",
    )(*units, little)
    return out[:-1], out[-1]


def body(
    images_in,
    crop_lengths,
    route_index,
    router_weight,
    norm_gain,
    norm_shift,
    qkv_weight,
    qv_bias,
    out_weight,
    out_bias,
    fc1_weight,
    fc1_bias,
    fc2_weight,
    fc2_bias,
    out_cotangent,
):
    own_count, length, features = images_in.shape
    width = qkv_weight.shape[-1]
    hidden = fc1_weight.shape[-1]
    group = lax.axis_size("tensor")

    qkv_rows = jnp.swapaxes(qkv_weight, 2, 3).reshape(2, 3 * width, features)
    attn_own = jnp.concatenate([qkv_rows, out_weight], axis=1)
    small = jnp.concatenate([qv_bias.reshape(1, -1), fc1_bias.reshape(1, -1)], axis=1).astype(F32)
    got, small = gather_weights(attn_own, fc1_weight, fc2_weight, small)
    w_attn = [(attn_own, got["attn", i]) for i in range(2)]
    w_ffn = [(fc1_weight, got["fc1", i], fc2_weight, got["fc2", i]) for i in range(2)]
    small = small.reshape(group, -1)
    qv_all = small[:, : 4 * width].reshape(group, 2, 2, 1, width)
    b1_all = small[:, 4 * width :].reshape(group, 2, 1, hidden)
    q_bias = [qv_all[:, i, 0] for i in range(2)]
    v_bias = [qv_all[:, i, 1] for i in range(2)]
    b1 = [b1_all[:, i] for i in range(2)]

    gains = norm_gain.astype(F32).reshape(4, 1, features)
    shifts = norm_shift.astype(F32).reshape(4, 1, features)
    o_bias = out_bias.astype(F32).reshape(2, 1, features)
    f_bias = fc2_bias.astype(F32).reshape(2, 1, features)

    mine = lax.axis_index("tensor") * own_count
    bounds = jnp.cumsum(lax.dynamic_slice_in_dim(crop_lengths, mine, 1, 0)[0])
    route = lax.dynamic_slice_in_dim(route_index, mine, 1, 0)[0]
    positions = jnp.arange(length, dtype=jnp.int32)

    def crops_of(places):
        column = jnp.sum((places[:, None] >= bounds[None, :]).astype(jnp.int32), axis=1)[:, None]
        line = jnp.sum((places[None, :] >= bounds[:, None]).astype(jnp.int32), axis=0)[None, :]
        return column, line

    crops_full, crops_chosen = crops_of(positions), crops_of(route)
    pick = route[:, None] == positions[None, :]
    pick_low, pick_full = pick.astype(BF16), pick.astype(F32)
    highest = lax.Precision.HIGHEST

    image = images_in[0]
    cotangent = out_cotangent[0]
    chosen = mm(pick_low, image, NN)
    router_data = router_weight.astype(F32)
    rate = 1.0 / (1.0 + jnp.exp(-jnp.sum(chosen * router_data[None, :], axis=1, keepdims=True)))

    forward_order = tuple(range(group))
    back_order = tuple(reversed(range(group)))

    res = attention_forward(
        chosen, gains[0], shifts[0], crops_chosen, (q_bias[0], v_bias[0]), o_bias[0],
        0, w_attn[0], forward_order,
    )
    middle, saved_one = res[0], res[1:]
    branches = (
        ffn_forward(
            middle, gains[1], shifts[1], b1[0], f_bias[0], 0, w_ffn[0], forward_order
        )
        - chosen
    )
    routed = image.astype(F32) + lax.dot_general(
        pick_full, rate * branches, TN, precision=highest, preferred_element_type=F32
    )
    res = attention_forward(
        routed, gains[2], shifts[2], crops_full, (q_bias[1], v_bias[1]), o_bias[1],
        1, w_attn[1], forward_order,
    )
    after_attn, saved_two = res[0], res[1:]

    res = ffn_both(
        after_attn, cotangent, gains[3], shifts[3], b1[1], f_bias[1], 1, w_ffn[1],
        back_order, True,
    )
    g_after, gain_four, shift_four, f_bias_two, b1_two, images_out = res[:6]
    fc1_two, fc2_two = res[6:]

    res = attention_backward(
        g_after, routed, gains[2], shifts[2], crops_full, saved_two, 1, w_attn[1], back_order
    )
    g_routed, gain_three, shift_three, o_bias_two, q_two, v_two = res[:6]
    attn_two = res[6]

    g_chosen = lax.dot_general(
        pick_full, g_routed, NN, precision=highest, preferred_element_type=F32
    )
    g_logit = jnp.sum(g_chosen * branches, axis=1, keepdims=True) * rate * (1.0 - rate)
    router_part = jnp.sum(chosen * g_logit, axis=0, keepdims=True)
    g_branch = rate * g_chosen
    res = ffn_both(
        middle, g_branch, gains[1], shifts[1], b1[0], f_bias[0], 0, w_ffn[0], back_order,
        False,
    )
    g_middle, gain_two, shift_two, f_bias_one, b1_one = res[:5]
    fc1_one, fc2_one = res[5:]

    res = attention_backward(
        g_middle, chosen, gains[0], shifts[0], crops_chosen, saved_one, 0, w_attn[0],
        back_order,
    )
    g_all, gain_one, shift_one, o_bias_one, q_one, v_one = res[:6]
    attn_one = res[6]

    own_grad = g_logit * router_data[None, :] + (g_all - g_branch)
    input_grad = g_routed + lax.dot_general(
        pick_full, own_grad, TN, precision=highest, preferred_element_type=F32
    )

    shared = jnp.concatenate(
        [
            router_part, gain_one, gain_two, gain_three, gain_four, shift_one, shift_two,
            shift_three, shift_four, o_bias_one, o_bias_two, f_bias_one, f_bias_two,
        ],
        axis=0,
    )
    blocked = jnp.concatenate([q_one, v_one, q_two, v_two, b1_one, b1_two], axis=2)
    blocked = blocked.reshape(group, -1, features)
    n_blocked = blocked.shape[1]
    little = jnp.concatenate(
        [
            jnp.pad(shared, ((0, 3), (0, 0))),
            jnp.pad(blocked, ((0, 0), (0, 8 - n_blocked), (0, 0))).reshape(8 * group, features),
        ],
        axis=0,
    )
    sums, little = reduce_gradients([fc1_two, fc2_two, attn_two, fc1_one, fc2_one, attn_one], little)
    fc1_two, fc2_two, attn_two, fc1_one, fc2_one, attn_one = sums
    shared, blocked = little[:13], little[16 : 16 + n_blocked].reshape(1, -1)

    def attention_grads(total):
        total = total.astype(F32)
        qkv = jnp.swapaxes(total[: 3 * width].reshape(3, width, features), 1, 2)
        return qkv, total[3 * width :]

    qkv_one, out_one = attention_grads(attn_one)
    qkv_two, out_two = attention_grads(attn_two)
    return (
        images_out[None],
        input_grad[None],
        shared[0],
        shared[1:5].reshape(2, 2, features),
        shared[5:9].reshape(2, 2, features),
        jnp.stack([qkv_one, qkv_two]),
        blocked[0, : 4 * width].reshape(2, 2, width),
        jnp.stack([out_one, out_two]),
        shared[9:11],
        jnp.stack([fc1_one, fc1_two]).astype(F32),
        blocked[0, 4 * width :].reshape(2, hidden),
        jnp.stack([fc2_one, fc2_two]).astype(F32),
        shared[11:13],
    )


def solution(mesh):
    in_specs = (
        P(("dp", "tensor"), None, None),
        P("dp", None),
        P("dp", None),
        P(),
        P(),
        P(),
        P(None, None, None, "tensor"),
        P(None, None, "tensor"),
        P(None, "tensor", None),
        P(),
        P(None, None, "tensor"),
        P(None, "tensor"),
        P(None, "tensor", None),
        P(),
        P(("dp", "tensor"), None, None),
    )
    out_specs = (
        P(("dp", "tensor"), None, None),
        P(("dp", "tensor"), None, None),
        P(),
        P(),
        P(),
        P(None, None, None, "tensor"),
        P(None, None, "tensor"),
        P(None, "tensor", None),
        P(),
        P(None, None, "tensor"),
        P(None, "tensor"),
        P(None, "tensor", None),
        P(),
    )
    return jax.shard_map(body, mesh=mesh, in_specs=in_specs, out_specs=out_specs, check_vma=False)
```

time: 1090 us -> 506 us (0.46)
  waiting for transfers between devices: 626 us -> 0 us
  Pallas kernels: 0 us -> 449 us
  matrix products: 193 us -> 13.5 us
  blocking collectives: 87.3 us -> 0 us
  other arithmetic: 80 us -> 15.2 us
  local copies, waits for them, and re-layouts: 77.8 us -> 22.8 us
  between operations: 16.2 us -> 1.69 us
    pallas_call x0 -> x9, Pallas kernels: none -> 449 us  [the longest x1 209 us: reduce_gradients(): pl.pallas_call(functools.partial(reduce_kernel, n_data, len(units), chunk...]
    reduce_scatter x8 -> x0, waiting for transfers between devices: 266 us -> none  [the longest x2 97.4 us: dense_back(): lax.psum_scatter(second_part.astype(jnp.bfloat16), 'tensor', scatter_dime...]
    all_gather x8 -> x0, waiting for transfers between devices: 211 us -> none  [the longest x2 74.4 us: dense_forward(): lax.all_gather(first_weights, 'tensor', axis=1, tiled=True)]
    dot_general x68 -> x4, matrix products: 193 us -> 13.5 us  [the longest x1 4.19 us: body(): lax.dot_general(pick_full, own_grad, TN, precision=highest, preferred_ele...]
    psum x1 -> x0, waiting for transfers between devices: 148 us -> none  [body(): lax.psum(qkv_part.astype(jnp.bfloat16), 'dp').astype(jnp.float32)]
    psum x2 -> x0, blocking collectives: 65 us -> none  [the longest x1 41.6 us: body(): lax.psum((router_part, gain_part, shift_part, out_bias_part, second_bias_...]
    gather x5 -> x0, local copies, waits for them, and re-layouts: 27.5 us -> none  [the longest x1 13.7 us: body(): chosen = images_in[row_index, own_index]]
    reduce_sum x27 -> x6, other arithmetic: 27.1 us -> 1.94 us  [the longest x1 1.47 us: body(): jnp.sum(chosen * router_data[None, :], axis=1, keepdims=True)]
  transfers between devices with their start and end apart: 17 -> 0, of which waited for: 14 -> 0; matrix products, arithmetic and copies ran while one was open for 14% -> 0% of each run, Pallas kernels for 0% -> 0%
where the time goes in v1:
time: 506 us; the launch traced here: 502 us
  Pallas kernels  449 us (89%)
  local copies, waits for them, and re-layouts  22.8 us (5%)
  other arithmetic  15.2 us (3%)
  matrix products  13.5 us (3%)
    pallas_call x1, Pallas kernels, reduce_gradients(): pl.pallas_call(functools.partial(reduce_kernel, n_data, len(units), chunk...  209 us
    pallas_call x2, Pallas kernels, ffn_both(): pl.pallas_call(kernel, out_shape=out_shape, grid_spec=pl.GridSpec(grid=(c...  72.6 us
    pallas_call x1, Pallas kernels, gather_weights(): pl.pallas_call(functools.partial(gather_kernel, n_data, units), out_shape...  69.7 us
    pallas_call x2, Pallas kernels, attention_backward(): pl.pallas_call(kernel, out_shape=[jax.ShapeDtypeStruct((length, features)...  53.5 us
    pallas_call x2, Pallas kernels, attention_forward(): pl.pallas_call(kernel, out_shape=[jax.ShapeDtypeStruct((length, features)...  31.9 us
    pallas_call x1, Pallas kernels, ffn_forward(): pl.pallas_call(kernel, out_shape=jax.ShapeDtypeStruct((length, features),...  12.1 us

profile of v1, /device:TPU:0, one launch (start us, length us, event | category | flops | bytes accessed | tf_op | source)
XLA Modules:
  0.0 502.3 jit_solution(3727230546408100662)
XLA Ops:
  0.7 0.8 dynamic-slice_bitcast_fusion
  1.8 0.6 broadcast_in_dim.15.refs_4_.refs_5_
  2.4 0.8 concatenate.28
  3.2 0.7 convert_element_type.48
  4.0 0.6 broadcast_in_dim.17.refs_4_.refs_5_
  4.7 0.7 copy.54
  5.3 0.6 maximum_convert_fusion.2.small
  6.0 1.3 fusion.17
  7.3 1.4 fusion.16
  8.7 0.7 reshape.184
  9.4 0.7 reshape.186
  10.1 0.6 slice_bitcast_fusion.9
  10.7 0.8 broadcast_in_dim.39.refs_3_.refs_4_
  11.4 0.8 broadcast_in_dim.40.refs_3_.refs_4_
  12.3 2.6 fusion.refs_0_.refs_1_
  14.9 2.6 pad_maximum_fusion.1.attn.refs_8_.refs_10_
  17.5 69.7 %gather_weights.1 = (bf16[3,768,768]{2,1,0:T(8,128)(2,1)}, bf16[3,768,768]{2,1,0:T(8,128)(2,1)}, bf16[3,768,768]{2,1,0:T(8,128)(2,1)}, bf16[3,768,768]{2,1,0:T(8...) custom-call(bf16[2,768,768]{2,1,0:T(8,128)(2,1)} %pad_maximum_fusion.1.attn.refs_8_.re, ...), custom_call_target="tpu_custom_call" | custom-call | tf_op jit(solution)/shard_map/gather_weights/pallas_call | solution.py:682
  87.2 0.8 copy.57
  88.1 0.6 slice_bitcast_fusion.2
  88.8 0.6 slice_bitcast_fusion.5
  89.4 12.0 %attention_forward.2 = (f32[272,768]{1,0:T(8,128)}, bf16[4,272,192]{2,1,0:T(8,128)(2,1)}, bf16[4,272,192]{2,1,0:T(8,128)(2,1)}, bf16[4,272,192]{2,1,0:T(8,128)(2,1)}, bf16[4,272,192]{2,1,0:T(8,128)(2,1)}) custom-call(f32[272,768]{1,0:T(8,128)} %fusion.refs_0_.refs_1_, f32[1,768]{1,0:T(1,128)} %get-tuple-element.145.refs_1_.refs_2_, ...), custom_call_target="tpu_custom_call" | custom-call | flops 1510735872 | bytes 8060928 | tf_op jit(solution)/shard_map/attention_forward/pallas_call | solution.py:152
  101.4 12.1 %ffn_forward.1 = f32[272,768]{1,0:T(8,128)} custom-call(f32[272,768]{1,0:T(8,128)} %get-tuple-element.68.refs_0_, f32[1,768]{1,0:T(1,128)} %get-tuple-element.146.refs_1_.refs_2_, f32[1,768]{1,0:T(1,128)} %get-tuple-element.135.refs_2_.refs_3_, f32[4,1,768]{2,1,0:T(1,128)} %get-tuple-element.128.refs_3_.refs_4_, ...), custom_call_target="tpu_custom_call" | custom-call | flops 2566914048 | bytes 11108352 | tf_op jit(solution)/shard_map/ffn_forward/pallas_call | solution.py:387
  113.6 1.5 multiply_reduce_fusion.2
  115.0 3.0 convert_add_fusion.refs_0_.refs_1_
  118.0 19.9 %attention_forward.3 = (f32[544,768]{1,0:T(8,128)}, bf16[4,544,192]{2,1,0:T(8,128)(2,1)}, bf16[4,544,192]{2,1,0:T(8,128)(2,1)}, bf16[4,544,192]{2,1,0:T(8,128)(2,1)}, bf16[4,544,192]{2,1,0:T(8,128)(2,1)}) custom-call(f32[544,768]{1,0:T(8,128)} %convert_add_fusion.refs_0_.refs_1_, f32[1,768]{1,0:T(1,128)} %get-tuple-element.147.refs_1_.refs_2_, ...), custom_call_target="tpu_custom_call" | custom-call | flops 3476029440 | bytes 11403264 | tf_op jit(solution)/shard_map/attention_forward/pallas_call | solution.py:152
  137.9 47.0 %ffn_both.1 = (f32[544,768]{1,0:T(8,128)}, f32[1,768]{1,0:T(1,128)}, f32[1,768]{1,0:T(1,128)}, f32[1,768]{1,0:T(1,128)}, f32[4,1,768]{2,1,0:T(1,128)}, /*index=5...) custom-call(f32[544,768]{1,0:T(8,128)} %get-tuple-element.72.refs_0_, ...), custom_call_target="tpu_custom_call" | custom-call | flops 15401484288 | bytes 23887872 | tf_op jit(solution)/shard_map/ffn_both/pallas_call | solution.py:522
  184.9 34.5 %attention_backward.2 = (f32[544,768]{1,0:T(8,128)}, f32[1,768]{1,0:T(1,128)}, f32[1,768]{1,0:T(1,128)}, f32[1,768]{1,0:T(1,128)}, f32[4,1,192]{2,1,0:T(1,128)},...) custom-call(f32[544,768]{1,0:T(8,128)} %get-tuple-element.76.refs_0_, f32[544,768]{1,0:T(8,128)} %convert_add_fusion.refs_0_.refs_1_, ...), custom_call_target="tpu_custom_call" | custom-call | flops 7406616576 | bytes 17793024 | tf_op jit(solution)/shard_map/attention_backward/pallas_call | solution.py:308
  219.4 3.7 multiply_reduce_fusion.1
  223.3 25.6 %ffn_backward.1 = (f32[272,768]{1,0:T(8,128)}, f32[1,768]{1,0:T(1,128)}, f32[1,768]{1,0:T(1,128)}, f32[1,768]{1,0:T(1,128)}, f32[4,1,768]{2,1,0:T(1,128)}, /*ind...) custom-call(f32[272,768]{1,0:T(8,128)} %get-tuple-element.68.refs_0_, f32[272,768]{1,0:T(8,128)} %get-tuple-element.120.refs_1_, ...), custom_call_target="tpu_custom_call" | custom-call | flops 6417285120 | bytes 21381120 | tf_op jit(solution)/shard_map/ffn_backward/pallas_call | solution.py:522
  249.0 19.0 %attention_backward.3 = (f32[272,768]{1,0:T(8,128)}, f32[1,768]{1,0:T(1,128)}, f32[1,768]{1,0:T(1,128)}, f32[1,768]{1,0:T(1,128)}, f32[4,1,192]{2,1,0:T(1,128)},...) custom-call(f32[272,768]{1,0:T(8,128)} %get-tuple-element.82.refs_0_, f32[272,768]{1,0:T(8,128)} %fusion.refs_0_.refs_1_, ...), custom_call_target="tpu_custom_call" | custom-call | flops 3135111168 | bytes 13615104 | tf_op jit(solution)/shard_map/attention_backward/pallas_call | solution.py:308
  268.2 4.2 add_bitcast_fusion
  272.8 0.7 select_maximum_fusion.refs_6_
  273.4 209.3 %reduce_gradients.1 = (bf16[768,768]{1,0:T(8,128)(2,1)}, bf16[768,768]{1,0:T(8,128)(2,1)}, bf16[768,768]{1,0:T(8,128)(2,1)}, bf16[768,768]{1,0:T(8,128)(2,1)}, b...) custom-call(bf16[4,768,768]{2,1,0:T(8,128)(2,1)} %get-tuple-element.88.refs_0_, ...), custom_call_target="tpu_custom_call" | custom-call | tf_op jit(solution)/shard_map/reduce_gradients/pallas_call | solution.py:914
  482.8 1.4 slice_reduce_fusion.2
  484.3 0.7 slice_bitcast_fusion.4
  485.1 0.6 reshape_squeeze.7
  485.7 0.7 reshape_squeeze.6
  486.3 1.4 fusion.14
  487.7 0.8 fusion.15
  488.6 0.6 reshape.179
  489.2 0.6 reshape.178
  489.8 1.3 slice.165
  491.3 1.0 copy-done.3
  492.5 2.0 pad_maximum_fusion
  494.8 1.1 pad_maximum_fusion.2
  495.9 0.5 copy-done.11
  496.8 2.5 maximum_convert_fusion
  499.3 2.5 maximum_convert_fusion.1
  (87 shorter events, 2.2 us)
Async XLA Ops:
  0.6 1.0 copy-start
  0.7 14.2 %copy-start.8 = (bf16[2,3,768,192]{2,3,1,0:T(8,128)(2,1)S(1)}, bf16[2,3,768,192]{2,3,1,0:T(8,128)(2,1)}, u32[]{:S(2)}) copy-start(bf16[2,3,768,192]{2,3,1,0:T(8,128)(2,1)} %param.21) | copy-start | bytes 5308420
  101.4 12.2 %copy-start.2 = (f32[272,768]{1,0:T(8,128)S(1)}, f32[272,768]{1,0:T(8,128)}, u32[]{:S(2)}) copy-start(f32[272,768]{1,0:T(8,128)} %fusion.refs_0_.refs_1_) | copy-start | bytes 2506756
  113.5 1.5 copy-start.7
  248.9 19.0 %copy-start.5 = (f32[544,768]{1,0:T(8,128)S(1)}, f32[544,768]{1,0:T(8,128)}, u32[]{:S(2)}) copy-start(f32[544,768]{1,0:T(8,128)} %get-tuple-element.81) | copy-start | bytes 5013508
  248.9 19.0 %copy-start.6 = (f32[272,768]{1,0:T(8,128)S(1)}, f32[272,768]{1,0:T(8,128)}, u32[]{:S(2)}) copy-start(f32[272,768]{1,0:T(8,128)} %get-tuple-element.120.refs_1_) | copy-start | bytes 2506756
  268.0 4.4 copy-start.13
  268.0 4.4 copy-start.14
  268.0 4.4 copy-start.15
  268.0 4.4 copy-start.16
  268.0 4.4 copy-start.17
  268.0 4.4 copy-start.18
  268.0 4.5 copy-start.19
  268.0 4.5 copy-start.20
  268.0 4.5 copy-start.21
  268.1 4.5 copy-start.22
  268.1 4.5 copy-start.23
  268.1 4.5 copy-start.24
  268.1 4.5 copy-start.25
  268.1 4.5 copy-start.26
  268.1 4.5 copy-start.27
  268.1 4.5 copy-start.28
  268.1 4.5 copy-start.29
  268.1 4.5 copy-start.30
  482.8 8.3 %copy-start.4 = (bf16[768,768]{1,0:T(8,128)(2,1)S(1)}, bf16[768,768]{1,0:T(8,128)(2,1)}, u32[]{:S(2)}) copy-start(bf16[768,768]{1,0:T(8,128)(2,1)} %get-tuple-element.113) | copy-start | bytes 3538948
  491.1 1.3 copy-start.3
  494.7 1.7 copy-start.11
  494.7 2.0 copy-start.12
  496.8 2.5 copy-start.9
  496.8 2.6 copy-start.10
  496.8 5.1 %copy-start.1 = (s32[4,272]{1,0:T(4,128)S(1)}, s32[4,272]{1,0:T(4,128)}, u32[]{:S(2)}) copy-start(s32[4,272]{1,0:T(4,128)} %param.17) | copy-start | bytes 13060
